TPU v7x, 512 devices: a whole 4x4x16 slice. The times are simulated.
512 devices in a mesh: dp: 8 (over x, z_hi), row: 8 (over y, core), col: 8 (over z_lo).
Axes of the slice: x: 4, y: 4, z: 16 (z_hi: 2, z_lo: 8; z = z_hi * 8 + z_lo), core: 2. Of those that a mesh axis runs over, the one named last changes fastest.
Arguments:
- inputs: bfloat16 [8, 1024, 4096], P('dp', 'col', 'row'), may hold values from -6 to 6
- weights: bfloat16 [4096, 3, 4096], P('row', None, 'col'), may hold values from -0.09375 to 0.09375
- feature_taps: float32 [3, 3, 4096], P(None, None, 'col'), may hold values from -2.5 to 2.5
- inner_taps: float32 [7, 4096], P(None, 'col'), may hold values from -2.5 to 2.5
- grad_out: bfloat16 [8, 1024, 4096], P('dp', 'row', 'col'), may hold values from -6 to 6
Outputs:
- grad_in: bfloat16 [8, 1024, 4096], P('dp', 'col', 'row')
- grad_weights: float32 [4096, 3, 4096], P('row', None, 'col')
All inputs are finite; a program needn't handle non-finite values.
Results may differ from a plain program's by a relative error of at most 0.033.
Values may be sent and summed in bfloat16 or wider, within the bound.
A program may use at most 64 MiB of HBM per device.

v0:
```python
import jax
import jax.numpy as jnp
from jax import lax
from jax.sharding import PartitionSpec as P


def with_halo(cells, sides, width):
    for axis, dim in sides:
        count = lax.axis_size(axis)
        ends = count - 1
        head = lax.slice_in_dim(cells, 0, width, axis=dim)
        tail = lax.slice_in_dim(cells, cells.shape[dim] - width, cells.shape[dim], axis=dim)
        cells = jnp.concatenate(
            [
                lax.ppermute(tail, axis, [(i, (i + 1) % count) for i in range(ends)]),
                cells,
                lax.ppermute(head, axis, [((i + 1) % count, i) for i in range(ends)]),
            ],
            axis=dim,
        )
    return cells


def shifted(shard, axis, by):
    length = lax.axis_size(axis)
    pairs = [(i, i + by) for i in range(length) if 0 <= i + by < length]
    return lax.ppermute(shard, axis, pairs)


def causal(seq, taps):
    total = taps[0] * seq
    for lag in range(1, taps.shape[0]):
        pad = jnp.zeros((lag,) + seq.shape[1:], jnp.float32)
        total = total + taps[lag] * jnp.concatenate([pad, seq[:-lag]], axis=0)
    return total


def anticausal(seq, taps):
    total = taps[0] * seq
    for lag in range(1, taps.shape[0]):
        pad = jnp.zeros((lag,) + seq.shape[1:], jnp.float32)
        total = total + taps[lag] * jnp.concatenate([seq[lag:], pad], axis=0)
    return total


def rounded(value):
    return lax.optimization_barrier(value.astype(jnp.bfloat16)).astype(jnp.float32)


def on_device(inputs, weights, feature_taps, inner_taps, grad_out):
    tile = inputs[0]
    upstream_tile = grad_out[0]
    rows_dev = upstream_tile.shape[0]
    width_row = weights.shape[0]
    width_col = weights.shape[2]
    margin = feature_taps.shape[0] - 1 + (inner_taps.shape[0] - 1)
    flat_w = weights.reshape(width_row, 3 * width_col)
    columns = lax.all_gather(tile, "col", axis=0, tiled=True)
    block = columns
    proj = lax.psum_scatter(
        jnp.dot(block, flat_w, preferred_element_type=jnp.float32).astype(jnp.bfloat16),
        "row",
        scatter_dimension=0,
        tiled=True,
    )
    padded = with_halo(proj, (("row", 0),), margin)
    after = shifted(upstream_tile[:margin], "row", -1)
    length = rows_dev + 2 * margin
    window = padded.astype(jnp.float32).reshape(length, 3, width_col)
    upstream = jnp.concatenate(
        [
            jnp.zeros((margin, width_col), jnp.float32),
            upstream_tile.astype(jnp.float32),
            after.astype(jnp.float32),
        ],
        axis=0,
    )
    mixed = causal(window, feature_taps)
    query = mixed[:, 0]
    key = mixed[:, 1]
    value = mixed[:, 2]
    product = rounded(key * value)
    inner = causal(product, inner_taps)
    grad_query = upstream * inner
    grad_inner = upstream * query
    grad_product = anticausal(grad_inner, inner_taps)
    grad_mixed = jnp.stack([grad_query, grad_product * value, grad_product * key], axis=1)
    grad_proj = anticausal(grad_mixed, feature_taps)[margin : margin + rows_dev].astype(
        jnp.bfloat16
    )
    gathered = lax.all_gather(grad_proj.reshape(rows_dev, 3 * width_col), "row", axis=0, tiled=True)
    block = gathered
    grad_x = lax.psum_scatter(
        lax.dot_general(
            block, flat_w, (((1,), (1,)), ((), ())), preferred_element_type=jnp.float32
        ).astype(jnp.bfloat16),
        "col",
        scatter_dimension=0,
        tiled=True,
    )
    local = lax.dot_general(
        columns, gathered, (((0,), (0,)), ((), ())), preferred_element_type=jnp.float32
    )
    grad_w = lax.psum(local.astype(jnp.bfloat16), "dp").astype(jnp.float32)
    return (grad_x[None], grad_w.reshape(width_row, 3, width_col))


def solution(mesh):
    placed = (
        P("dp", "col", "row"),
        P("row", None, "col"),
        P(None, None, "col"),
        P(None, "col"),
        P("dp", "row", "col"),
    )
    return jax.shard_map(
        on_device,
        mesh=mesh,
        in_specs=placed,
        out_specs=(P("dp", "col", "row"), P("row", None, "col")),
        check_vma=False,
    )
```

profile of v0, /device:TPU:2, one launch (start us, length us, event | category | flops | bytes accessed | tf_op | source)
XLA Modules:
  0.0 570.3 jit_solution(13624536837322378949)
XLA Ops:
  7.2 0.7 all-gather.6.cloned.1.call-update
  7.9 1.7 copy.13
  9.7 72.4 %all-gather.6.cloned.1.call-done = bf16[1,1024,512]{2,1,0:T(8,128)(2,1)} async-done(((bf16[1,128,512]{2,1,0:T(8,128)(2,1)}), bf16[1,1024,512]{2,1,0:T(8,128)(2,1)}) %all-gather.6.cloned.1.call-update) | async-done | bytes 1048592 | tf_op jit(solution)/shard_map/all_gather | solution.py:58
  82.0 4.7 convolution_convert_fusion
  86.8 0.8 copy-done.3
  87.8 1.3 collective-permute-start
  89.1 34.9 %reduce-scatter.3.cloned.1.call-done = bf16[128,1536]{1,0:T(8,128)(2,1)} async-done(((bf16[1024,1536]{1,0:T(8,128)(2,1)}), bf16[128,1536]{1,0:T(8,128)(2,1)}) %reduce-scatter.3.cloned.1.call-update) | async-done | bytes 393232 | tf_op jit(solution)/shard_map/reduce_scatter | solution.py:60
  124.0 0.8 fusion.6
  124.8 1.3 collective-permute-start.2
  126.1 3.0 collective-permute-start.1
  129.3 1.2 copy.14
  130.6 0.5 copy.21
  131.1 1.6 copy.20
  132.7 0.2 copy.16
  132.9 0.2 copy.15
  133.2 3.2 multiply_add_fusion
  136.4 0.3 fusion.5
  136.8 0.2 slice.173
  137.0 0.2 slice.172
  137.9 0.8 multiply_bitcast_fusion.1
  139.0 1.8 multiply_bitcast_fusion.2
  140.9 0.5 slice.176
  141.4 0.5 slice.175
  141.9 2.1 fusion.3
  144.0 39.5 %all-gather.4.cloned.1.call-done = bf16[1024,1536]{0,1:T(8,128)(2,1)} async-done(((bf16[128,1536]{0,1:T(8,128)(2,1)}), bf16[1024,1536]{0,1:T(8,128)(2,1)}) %all-gather.4.cloned.1.call-update) | async-done | bytes 3145744 | tf_op jit(solution)/shard_map/all_gather | solution.py:91
  183.6 3.7 convolution_convert_fusion.1
  187.3 1.6 copy.19
  188.9 1.3 copy-done.2
  190.2 4.7 convolution_convert_fusion.2
  194.9 296.3 %all-reduce.18.cloned.1.call-done = bf16[512,3,512]{2,0,1:T(8,128)(2,1)} async-done(((bf16[512,3,512]{2,0,1:T(8,128)(2,1)}), bf16[512,3,512]{2,0,1:T(8,128)(2,1)}) %all-reduce.18.cloned.1.call-update) | async-done | bytes 1572880 | tf_op jit(solution)/shard_map/psum | solution.py:104
  491.3 3.5 reshape.28
  494.8 68.9 %reduce-scatter.5.cloned.1.call-done = bf16[128,512]{1,0:T(8,128)(2,1)} async-done(((bf16[1024,512]{1,0:T(8,128)(2,1)}), bf16[128,512]{1,0:T(8,128)(2,1)}) %reduce-scatter.5.cloned.1.call-update) | async-done | bytes 131088 | tf_op jit(solution)/shard_map/reduce_scatter | solution.py:93
  (45 shorter events, 1.8 us)
Async XLA Ops:
  7.2 74.9 %all-gather.6.cloned.1.call-start = ((), (), s32[]{:S(2)}) async-start(), calls=%async_computation.6 | async-start | bytes 1179648 | tf_op jit(solution)/shard_map/all_gather | solution.py:58
  7.9 116.1 %reduce-scatter.3.cloned.1.call-start = ((), (), s32[]{:S(2)}) async-start(), calls=%async_computation.2 | async-start | bytes 3538944 | tf_op jit(solution)/shard_map/reduce_scatter | solution.py:60
  9.7 77.1 %copy-start.1 = (bf16[512,3,512]{0,2,1:T(8,128)(2,1)}, bf16[512,3,512]{0,2,1:T(8,128)(2,1)S(1)}, u32[]{:S(2)}) copy-start(bf16[512,3,512]{0,2,1:T(8,128)(2,1)S(1)} %copy.13) | copy-start | bytes 4718596
  86.8 0.9 copy-start.3
  86.8 2.3 copy-start.4
  86.8 42.4 %copy-start.5 = (f32[7,512]{1,0:T(8,128)S(1)}, f32[7,512]{1,0:T(8,128)}, u32[]{:S(2)}) copy-start(f32[7,512]{1,0:T(8,128)} %param.8) | copy-start | bytes 43012
  86.8 96.8 %all-gather.4.cloned.1.call-start = ((), (), s32[]{:S(2)}) async-start(), calls=%async_computation.3 | async-start | bytes 3538944 | tf_op jit(solution)/shard_map/all_gather | solution.py:91
  87.8 41.4 %collective-permute-start = (bf16[8,512]{0,1:T(8,128)(2,1)S(1)}, bf16[8,512]{0,1:T(8,128)(2,1)S(1)}, u32[]{:S(2)}, u32[]{:S(2)}) collective-permute-start(bf16[8,512]{0,1:T(8,128)(2,1)S(1)} %slice_bitcast_fusion.3), channel_id=1, source_target_pairs={{8,0},{16,8},{24,16},{32,24},{40,32},{48,40},{56,48},{9,1},{17,9},... | collective-permute-start | bytes 24584 | tf_op jit(solution)/shard_map/ppermute | solution.py:27
  124.0 6.5 %copy-start = (bf16[128,1536]{1,0:T(8,128)(2,1)S(1)}, bf16[128,1536]{1,0:T(8,128)(2,1)}, u32[]{:S(2)}) copy-start(bf16[128,1536]{1,0:T(8,128)(2,1)} %reduce-scatter.3.cloned.1.call-done) | copy-start | bytes 1179652
  124.8 5.6 collective-permute-start.2
  126.1 4.4 collective-permute-start.1
  141.9 41.7 %copy-start.6 = (bf16[1,1024,512]{2,1,0:T(8,128)(2,1)S(1)}, bf16[1,1024,512]{2,1,0:T(8,128)(2,1)}, u32[]{:S(2)}) copy-start(bf16[1,1024,512]{2,1,0:T(8,128)(2,1)} %all-gather.6.cloned.1.call-done) | copy-start | bytes 3145732
  144.0 347.3 %all-reduce.18.cloned.1.call-start = ((), (), s32[]{:S(2)}) async-start(), calls=%async_computation.5 | async-start | bytes 3145728 | tf_op jit(solution)/shard_map/psum | solution.py:104
  188.8 1.4 copy-start.2
  188.9 374.9 %reduce-scatter.5.cloned.1.call-start = ((), (), s32[]{:S(2)}) async-start(), calls=%async_computation.4 | async-start | bytes 1179648 | tf_op jit(solution)/shard_map/reduce_scatter | solution.py:93
Sparse Core Ops, SparseCore 0:
  10.1 71.9 all-gather.5
  86.9 37.0 reduce-scatter.2
  144.1 39.4 all-gather.3
  189.0 302.2 all-reduce.17
  494.5 69.1 reduce-scatter.4
where the time goes:
time: 571 us; the launch traced here: 570 us
  waiting for transfers between devices  513 us (90%)
  between operations  14.1 us (2%)
  matrix products  13.1 us (2%)
  local copies, waits for them, and re-layouts  12.5 us (2%)
  other arithmetic  11.9 us (2%)
  starting transfers between devices  5.8 us (1%)
    psum x1, waiting for transfers between devices, on_device(): grad_w = lax.psum(local.astype(jnp.bfloat16), 'dp').astype(jnp.float32)  296 us
    all_gather x1, waiting for transfers between devices, on_device(): columns = lax.all_gather(tile, 'col', axis=0, tiled=True)  72.4 us
    reduce_scatter x1, waiting for transfers between devices, on_device(): lax.psum_scatter(lax.dot_general(block, flat_w, (((1,), (1,)), ((), ())),...  68.9 us
    all_gather x1, waiting for transfers between devices, on_device(): lax.all_gather(grad_proj.reshape(rows_dev, 3 * width_col), 'row', axis=0,...  39.5 us
    reduce_scatter x1, waiting for transfers between devices, on_device(): lax.psum_scatter(jnp.dot(block, flat_w, preferred_element_type=jnp.float3...  34.9 us
  transfers between devices with their start and end apart: 8, of which 5 were waited for; matrix products, arithmetic and copies ran while one was open for 2% of the time, Pallas kernels for 0%

commit v1 on v0

--- a/solution.py
+++ b/solution.py
@@ -1,7 +1,337 @@
+import functools
+
 import jax
 import jax.numpy as jnp
 from jax import lax
+from jax.experimental import pallas as pl
+from jax.experimental.pallas import tpu as pltpu
 from jax.sharding import PartitionSpec as P
+
+MESH = pl.DeviceIdType.MESH
+NT = (((1,), (1,)), ((), ()))
+CHUNKS = 6
+RING = 4
+F32 = jnp.float32
+BF16 = jnp.bfloat16
+
+
+class Place:
+    def __init__(self):
+        self.dp, self.row, self.col = (lax.axis_index(a) for a in ("dp", "row", "col"))
+        self.x, self.zh = self.dp // 2, self.dp % 2
+        self.y, self.core = self.row // 2, self.row % 2
+
+    def at_x(self, by):
+        return (((self.x + by + RING) % RING) * 2 + self.zh, self.row, self.col)
+
+    def at_y(self, by):
+        return (self.dp, ((self.y + by + RING) % RING) * 2 + self.core, self.col)
+
+    def sibling(self):
+        return (self.dp, self.y * 2 + 1 - self.core, self.col)
+
+    def at_z(self, by):
+        z = (self.zh * 8 + self.col + by + 16) % 16
+        return (self.x * 2 + z // 8, self.row, z % 8)
+
+    def at_col(self, by):
+        return (self.dp, self.row, (self.col + by + 8) % 8)
+
+
+def greet(partners):
+    barrier = pltpu.get_barrier_semaphore()
+    for partner in partners:
+        pl.semaphore_signal(barrier, inc=1, device_id=partner, device_id_type=MESH)
+    pl.semaphore_wait(barrier, len(partners))
+
+
+class Sends:
+    def __init__(self, sems):
+        self.sems, self.copies = sems, []
+
+    def start(self, src, dst, recv, device):
+        copy = pltpu.make_async_remote_copy(
+            src_ref=src, dst_ref=dst, send_sem=self.sems.at[len(self.copies)], recv_sem=recv,
+            device_id=device, device_id_type=MESH,
+        )
+        copy.start()
+        self.copies.append(copy)
+
+    def finish(self):
+        for copy in self.copies:
+            copy.wait_send()
+
+
+def arrived(ref, sem, place):
+    pltpu.make_async_copy(ref, ref, sem).wait()
+
+
+def tail_kernel(
+    gp, xg, w, gx, dw,
+    G, XT, D, xrel, xrec, S, zrel, zrec, rr, rl, part,
+    sends, col_send, g_recv, xrel_sem, xrec_sem, zrel_sem, zrec_sem, out_sem, rr_sem, rl_sem,
+):
+    me = Place()
+    rows = gp.shape[0]
+    half = rows // 2
+    wide = w.shape[2]
+    step = 3 * wide // CHUNKS
+    per = wide // step
+    right, left = me.at_y(1), me.at_y(-1)
+    sibling = me.sibling()
+    xr, xl = me.at_x(1), me.at_x(-1)
+    up, down = me.at_z(4), me.at_z(-4)
+    col_up, col_down = me.at_col(1), me.at_col(-1)
+    greet([right, left, sibling, xr, xl, up, down, col_up, col_down])
+    out = Sends(sends)
+
+    def g_at(slot, h):
+        return G.at[pl.ds(pl.multiple_of(slot * rows + h * half, half), half)]
+
+    def g_send(src, slot, h, device):
+        out.start(src, g_at(slot, h), g_recv.at[slot, h], device)
+
+    def g_wait(slot, h):
+        arrived(g_at(slot, h), g_recv.at[slot, h], me)
+
+    def same(by):
+        return ((me.y + by + RING) % RING) * 2 + me.core
+
+    def other(by):
+        return ((me.y + by + RING) % RING) * 2 + 1 - me.core
+
+    own = [gp.at[pl.ds(h * half, half)] for h in range(2)]
+    g_send(own[0], me.row, 0, right)
+    g_send(own[1], me.row, 1, left)
+    g_send(own[1], me.row, 1, right)
+    g_send(own[0], me.row, 0, left)
+    for h in range(2):
+        g_send(own[h], me.row, h, sibling)
+    G[pl.ds(pl.multiple_of(me.row * rows, rows), rows), :] = gp[...]
+    for b in range(8):
+        XT[:, b * rows : (b + 1) * rows] = xg[b * rows : (b + 1) * rows, :].T
+
+    @pl.when(me.col == 7)
+    def _():
+        rr[...] = jnp.zeros_like(rr)
+
+    @pl.when(me.col == 0)
+    def _():
+        rl[...] = jnp.zeros_like(rl)
+
+    g_wait(same(-1), 0)
+    g_send(g_at(same(-1), 0), same(-1), 0, right)
+    g_send(g_at(same(-1), 0), same(-1), 0, sibling)
+    g_wait(same(1), 1)
+    g_send(g_at(same(1), 1), same(1), 1, left)
+    g_send(g_at(same(1), 1), same(1), 1, sibling)
+    g_wait(same(-1), 1)
+    g_send(g_at(same(-1), 1), same(-1), 1, sibling)
+    g_wait(same(1), 0)
+    g_send(g_at(same(1), 0), same(1), 0, sibling)
+    g_wait(same(2), 0)
+    g_send(g_at(same(2), 0), same(2), 0, sibling)
+    g_wait(same(2), 1)
+    g_send(g_at(same(2), 1), same(2), 1, sibling)
+    for by in (0, -1, 1, 2):
+        for h in range(2):
+            g_wait(other(by), h)
+
+    def grad_in_of(block):
+        at = pl.ds(pl.multiple_of(block * rows, rows), rows)
+        total = lax.dot_general(G[at, 0:wide], w[0], NT, preferred_element_type=F32)
+        for c in range(1, 3):
+            total = total + lax.dot_general(
+                G[at, c * wide : (c + 1) * wide], w[c], NT, preferred_element_type=F32
+            )
+        return total
+
+    def col_copy(block, side):
+        landing, sems, device = ((rr, rr_sem, col_down), (rl, rl_sem, col_up))[side]
+        return pltpu.make_async_remote_copy(
+            src_ref=part.at[block], dst_ref=landing.at[block], send_sem=col_send.at[block],
+            recv_sem=sems.at[block], device_id=device, device_id_type=MESH,
+        )
+
+    def col_round(s):
+        @pl.when(s + me.col >= 7)
+        def _():
+            block = s + me.col - 7
+
+            @pl.when(me.col < 7)
+            def _():
+                arrived(rr.at[block], rr_sem.at[block], me)
+
+            part[block] = (grad_in_of(block) + rr[block].astype(F32)).astype(BF16)
+            col_copy(block, 0).start()
+
+        @pl.when(s >= me.col)
+        def _():
+            block = 7 - s + me.col
+
+            @pl.when(me.col > 0)
+            def _():
+                arrived(rl.at[block], rl_sem.at[block], me)
+
+            part[block] = (grad_in_of(block) + rl[block].astype(F32)).astype(BF16)
+            col_copy(block, 1).start()
+
+    def col_last():
+        total = grad_in_of(me.col)
+
+        @pl.when(me.col < 7)
+        def _():
+            arrived(rr.at[me.col], rr_sem.at[me.col], me)
+
+        @pl.when(me.col > 0)
+        def _():
+            arrived(rl.at[me.col], rl_sem.at[me.col], me)
+
+        gx[...] = (total + rr[me.col].astype(F32) + rl[me.col].astype(F32)).astype(BF16)
+
+        for block in range(8):
+
+            @pl.when(block < me.col)
+            def _():
+                col_copy(block, 0).wait_send()
+
+            @pl.when(block > me.col)
+            def _():
+                col_copy(block, 1).wait_send()
+
+    top, bottom = pl.ds(0, half), pl.ds(half, half)
+    halves = (top, bottom)
+    to_r, to_l, to_o = ((me.x + by + RING) % RING for by in (1, 3, 2))
+
+    def dw_at(q, h, m):
+        return dw.at[
+            m // per,
+            pl.ds(pl.multiple_of(q * rows + h * half, half), half),
+            pl.ds((m % per) * step, step),
+        ]
+
+    def multiply(m):
+        for q in range(RING):
+            D[q, m] = jnp.dot(
+                XT[q * rows : (q + 1) * rows, :], G[:, m * step : (m + 1) * step],
+                preferred_element_type=F32,
+            ).astype(BF16)
+        out.start(D.at[to_o, m, top], xrel.at[0, m], xrel_sem.at[0, m], xr)
+        out.start(D.at[to_o, m, bottom], xrel.at[1, m], xrel_sem.at[1, m], xl)
+        out.start(D.at[to_r, m, bottom], xrec.at[0, m, bottom], xrec_sem.at[0, 1, m], xr)
+        out.start(D.at[to_l, m, top], xrec.at[1, m, top], xrec_sem.at[1, 0, m], xl)
+
+    def relay_x(m):
+        arrived(xrel.at[0, m], xrel_sem.at[0, m], me)
+        D[to_r, m, top] = (D[to_r, m, top].astype(F32) + xrel[0, m].astype(F32)).astype(BF16)
+        out.start(D.at[to_r, m, top], xrec.at[0, m, top], xrec_sem.at[0, 0, m], xr)
+        arrived(xrel.at[1, m], xrel_sem.at[1, m], me)
+        D[to_l, m, bottom] = (D[to_l, m, bottom].astype(F32) + xrel[1, m].astype(F32)).astype(BF16)
+        out.start(D.at[to_l, m, bottom], xrec.at[1, m, bottom], xrec_sem.at[1, 1, m], xl)
+
+    def exchange(m):
+        for side in range(2):
+            for h in range(2):
+                arrived(xrec.at[side, m, halves[h]], xrec_sem.at[side, h, m], me)
+        S[m] = (D[me.x, m].astype(F32) + xrec[0, m].astype(F32) + xrec[1, m].astype(F32)).astype(BF16)
+        out.start(S.at[m, top], zrel.at[0, m], zrel_sem.at[0, m], up)
+        out.start(S.at[m, bottom], zrel.at[1, m], zrel_sem.at[1, m], down)
+
+    def relay_z(m):
+        arrived(zrel.at[0, m], zrel_sem.at[0, m], me)
+        out.start(zrel.at[0, m], zrec.at[m, top], zrec_sem.at[0, m], up)
+        arrived(zrel.at[1, m], zrel_sem.at[1, m], me)
+        out.start(zrel.at[1, m], zrec.at[m, bottom], zrec_sem.at[1, m], down)
+
+    def gather(q, h, m, device):
+        out.start(dw_at(q, h, m), dw_at(q, h, m), out_sem.at[q, h, m], device)
+
+    def gathered(q, h, m):
+        arrived(dw_at(q, h, m), out_sem.at[q, h, m], me)
+
+    def total_of(m):
+        for h in range(2):
+            arrived(zrec.at[m, halves[h]], zrec_sem.at[h, m], me)
+        dw[
+            m // per, pl.ds(pl.multiple_of(me.x * rows, rows), rows), pl.ds((m % per) * step, step)
+        ] = (S[m].astype(F32) + zrec[m].astype(F32)).astype(BF16)
+        gather(me.x, 0, m, xr)
+        gather(me.x, 1, m, xl)
+        gather(me.x, 1, m, xr)
+        gather(me.x, 0, m, xl)
+
+    def relay_out(m):
+        gathered(to_l, 0, m)
+        gather(to_l, 0, m, xr)
+        gathered(to_r, 1, m)
+        gather(to_r, 1, m, xl)
+
+    def last_out(m):
+        gathered(to_l, 1, m)
+        gathered(to_r, 0, m)
+        gathered(to_o, 0, m)
+        gathered(to_o, 1, m)
+
+    stages = [multiply, relay_x, exchange, relay_z, total_of, relay_out, last_out]
+    order = []
+    lag = [0, 2, 3, 5, 7, 8, 9]
+    for slot in range(CHUNKS + lag[-1]):
+        for k in reversed(range(len(stages))):
+            m = slot - lag[k]
+            if 0 <= m < CHUNKS:
+                order.append((stages[k], m))
+        if 1 <= slot < 8:
+            order.append((col_round, slot - 1))
+        if slot == 8:
+            order.append((lambda unused: col_last(), 0))
+    for stage, m in order:
+        stage(m)
+    out.finish()
+
+
+SENDS = 6 + 8 + CHUNKS * (4 + 2 + 2 + 2 + 4 + 2)
+
+
+def tail(gp, xg, w):
+    rows, wide = gp.shape[0], w.shape[2]
+    half, step = rows // 2, 3 * wide // CHUNKS
+    vmem, sem = pltpu.VMEM, pltpu.SemaphoreType.DMA
+    return pl.pallas_call(
+        tail_kernel,
+        out_shape=(
+            jax.ShapeDtypeStruct((rows, w.shape[1]), BF16),
+            jax.ShapeDtypeStruct(w.shape, BF16),
+        ),
+        in_specs=[pl.BlockSpec(memory_space=pltpu.VMEM)] * 3,
+        out_specs=(pl.BlockSpec(memory_space=pltpu.VMEM),) * 2,
+        scratch_shapes=[
+            vmem((8 * rows, 3 * wide), BF16),
+            vmem((w.shape[1], 8 * rows), BF16),
+            vmem((RING, CHUNKS, rows, step), BF16),
+            vmem((2, CHUNKS, half, step), BF16),
+            vmem((2, CHUNKS, rows, step), BF16),
+            vmem((CHUNKS, rows, step), BF16),
+            vmem((2, CHUNKS, half, step), BF16),
+            vmem((CHUNKS, rows, step), BF16),
+            vmem((8, rows, w.shape[1]), BF16),
+            vmem((8, rows, w.shape[1]), BF16),
+            vmem((8, rows, w.shape[1]), BF16),
+            sem((SENDS,)),
+            sem((8,)),
+            sem((8, 2)),
+            sem((2, CHUNKS)),
+            sem((2, 2, CHUNKS)),
+            sem((2, CHUNKS)),
+            sem((2, CHUNKS)),
+            sem((RING, 2, CHUNKS)),
+            sem((8,)),
+            sem((8,)),
+        ],
+        compiler_params=pltpu.CompilerParams(
+            collective_id=1, has_side_effects=True, vmem_limit_bytes=44 * 2**20
+        ),
+        name="tail",
+    )(gp, xg, w)
 
 
 def with_halo(cells, sides, width):
@@ -88,21 +418,10 @@
     grad_proj = anticausal(grad_mixed, feature_taps)[margin : margin + rows_dev].astype(
         jnp.bfloat16
     )
-    gathered = lax.all_gather(grad_proj.reshape(rows_dev, 3 * width_col), "row", axis=0, tiled=True)
-    block = gathered
-    grad_x = lax.psum_scatter(
-        lax.dot_general(
-            block, flat_w, (((1,), (1,)), ((), ())), preferred_element_type=jnp.float32
-        ).astype(jnp.bfloat16),
-        "col",
-        scatter_dimension=0,
-        tiled=True,
-    )
-    local = lax.dot_general(
-        columns, gathered, (((0,), (0,)), ((), ())), preferred_element_type=jnp.float32
-    )
-    grad_w = lax.psum(local.astype(jnp.bfloat16), "dp").astype(jnp.float32)
-    return (grad_x[None], grad_w.reshape(width_row, 3, width_col))
+    grad_x, grad_w = tail(
+        grad_proj.reshape(rows_dev, 3 * width_col), columns, weights.transpose(1, 0, 2)
+    )
+    return grad_x[None], grad_w.astype(jnp.float32).transpose(1, 0, 2)
 
 
 def solution(mesh):

time: 571 us -> 260 us (0.46)
  the two profiles are of different devices: /device:TPU:2 before, /device:TPU:8 now
where the time goes in v1:
time: 260 us; the launch traced here: 259 us
  Pallas kernels  108 us (42%)
  waiting for transfers between devices  104 us (40%)
  between operations  14.4 us (6%)
  local copies, waits for them, and re-layouts  10.6 us (4%)
  other arithmetic  9.88 us (4%)
  starting transfers between devices  7.55 us (3%)
  matrix products  4.72 us (2%)
    pallas_call x1, Pallas kernels, tail(): pl.pallas_call(tail_kernel, out_shape=(jax.ShapeDtypeStruct((rows, w.shap...  108 us
    all_gather x1, waiting for transfers between devices, on_device(): columns = lax.all_gather(tile, 'col', axis=0, tiled=True)  72.2 us
    reduce_scatter x1, waiting for transfers between devices, on_device(): lax.psum_scatter(jnp.dot(block, flat_w, preferred_element_type=jnp.float3...  31 us
  transfers between devices with their start and end apart: 5, of which 3 were waited for; matrix products, arithmetic and copies ran while one was open for 2% of the time, Pallas kernels for 0%

profile of v1, /device:TPU:8, one launch (start us, length us, event | category | flops | bytes accessed | tf_op | source)
XLA Modules:
  0.0 259.3 jit_solution(12521688917466321870)
XLA Ops:
  7.2 0.7 all-gather.3.cloned.1.call-update
  7.9 1.7 copy.13
  9.7 72.2 %all-gather.3.cloned.1.call-done = bf16[1,1024,512]{2,1,0:T(8,128)(2,1)} async-done(((bf16[1,128,512]{2,1,0:T(8,128)(2,1)}), bf16[1,1024,512]{2,1,0:T(8,128)(2,1)}) %all-gather.3.cloned.1.call-update) | async-done | bytes 1048592 | tf_op jit(solution)/shard_map/all_gather | solution.py:388
  81.9 4.7 %convolution_convert_fusion = bf16[1024,1536]{1,0:T(8,128)(2,1)} fusion(bf16[512,1536]{0,1:T(8,128)(2,1)S(1)} %bitcast.64, bf16[1,1024,512]{2,1,0:T(8,128)(2,1)} %all-gather.3.cloned.1.call-done), kind=kOutput, calls=%fused_computation | convolution fusion | flops 1612185600 | bytes 5767168 | tf_op jit(solution)/shard_map/dot_general | solution.py:391
  86.6 0.9 copy-done.3
  87.7 1.9 collective-permute-start
  89.6 31.0 %reduce-scatter.2.cloned.1.call-done = bf16[128,1536]{1,0:T(8,128)(2,1)} async-done(((bf16[1024,1536]{1,0:T(8,128)(2,1)}), bf16[128,1536]{1,0:T(8,128)(2,1)}) %reduce-scatter.2.cloned.1.call-update) | async-done | bytes 393232 | tf_op jit(solution)/shard_map/reduce_scatter | solution.py:390
  120.6 0.8 fusion.5
  121.5 1.9 collective-permute-start.1
  123.4 3.6 %collective-permute-start.2 = (bf16[8,1536]{1,0:T(8,128)(2,1)S(1)}, bf16[8,1536]{1,0:T(8,128)(2,1)S(1)}, u32[]{:S(2)}, u32[]{:S(2)}) collective-permute-start(bf16[8,1536]{1,0:T(8,128)(2,1)S(1)} %get-tuple-element.11), channel_id=1, source_target_pairs={{8,0},{16,8},{24,16},{32,24},{40,32},{48,40},{56,48},{9,1},{17,9},... | collective-permute-start | bytes 73736 | tf_op jit(solution)/shard_map/ppermute | solution.py:347
  127.1 1.2 copy.14
  128.6 0.5 copy.20
  129.1 1.6 copy.21
  130.7 0.2 copy.15
  130.9 0.2 copy.16
  131.2 3.2 %multiply_add_fusion = f32[144,3,512]{0,2,1:T(8,128)S(1)} fusion(f32[142,3,512]{0,2,1:T(8,128)} %bitcast.63, f32[143,3,512]{0,2,1:T(8,128)S(1)} %bitcast.62, bf16[8,3,512]{0,2,1:T(8,128)(2,1)S(1)} %copy.16, bf16[128,3,512]{0,2,1:T(8,128)(2,1)S(1)} %bitcast.65, bf16[8,3,512]{0,2,1:T(8,128)(2,1)S(1)} %copy.15, f32[3,512]{1,0:T(4,128)S(1)} %get-tuple-element.13, ...), kind=kLoop, calls=%fused_computation.3 | loop fusion | flops 2433024 | bytes 3096576 | tf_op jit(solution)/shard_map/add | solution.py:364
  134.4 0.3 fusion.3
  134.7 0.2 slice.169
  134.9 0.2 slice.170
  135.1 0.2 slice.171
  135.3 0.2 slice.172
  135.5 0.2 slice.173
  135.7 0.2 slice.174
  135.9 0.8 multiply_bitcast_fusion.1
  137.1 1.8 multiply_bitcast_fusion.2
  139.0 0.5 slice.175
  139.4 0.5 slice.176
  139.9 1.4 fusion.1
  141.3 0.2 copy.19.gp
  141.6 108.1 %tail.1 = (bf16[128,512]{1,0:T(8,128)(2,1)S(1)}, bf16[3,512,512]{2,1,0:T(8,128)(2,1)S(1)}) custom-call(bf16[128,1536]{1,0:T(8,128)(2,1)S(1)} %copy.19.gp, bf16[1024,512]{1,0:T(8,128)(2,1)S(1)} %bitcast.58, bf16[3,512,512]{2,1,0:T(8,128)(2,1)S(1)} %bitcast.57), custom_call_target="tpu_custom_call" | custom-call | tf_op jit(solution)/shard_map/tail/pallas_call | solution.py:299
  249.7 2.1 convert_bitcast_fusion
  251.8 0.7 copy.23
  (34 shorter events, 1.1 us)
Async XLA Ops:
  7.2 74.7 %all-gather.3.cloned.1.call-start = ((), (), s32[]{:S(2)}) async-start(), calls=%async_computation.2 | async-start | bytes 1179648 | tf_op jit(solution)/shard_map/all_gather | solution.py:388
  7.9 112.7 %reduce-scatter.2.cloned.1.call-start = ((), (), s32[]{:S(2)}) async-start(), calls=%async_computation.1 | async-start | bytes 3538944 | tf_op jit(solution)/shard_map/reduce_scatter | solution.py:390
  86.6 0.9 copy-start.3
  86.6 3.0 %copy-start.4 = (f32[3,3,512]{2,1,0:T(4,128)S(1)}, f32[3,3,512]{2,1,0:T(4,128)}, u32[]{:S(2)}) copy-start(f32[3,3,512]{2,1,0:T(4,128)} %param.7) | copy-start | bytes 55300
  86.6 40.4 %copy-start.5 = (f32[7,512]{1,0:T(8,128)S(1)}, f32[7,512]{1,0:T(8,128)}, u32[]{:S(2)}) copy-start(f32[7,512]{1,0:T(8,128)} %param.8) | copy-start | bytes 43012
  87.7 39.4 %collective-permute-start = (bf16[8,512]{0,1:T(8,128)(2,1)S(1)}, bf16[8,512]{0,1:T(8,128)(2,1)S(1)}, u32[]{:S(2)}, u32[]{:S(2)}) collective-permute-start(bf16[8,512]{0,1:T(8,128)(2,1)S(1)} %slice_bitcast_fusion.3), channel_id=1, source_target_pairs={{8,0},{16,8},{24,16},{32,24},{40,32},{48,40},{56,48},{9,1},{17,9},... | collective-permute-start | bytes 24584 | tf_op jit(solution)/shard_map/ppermute | solution.py:357
  120.6 7.9 %copy-start.2 = (bf16[128,1536]{1,0:T(8,128)(2,1)S(1)}, bf16[128,1536]{1,0:T(8,128)(2,1)}, u32[]{:S(2)}) copy-start(bf16[128,1536]{1,0:T(8,128)(2,1)} %reduce-scatter.2.cloned.1.call-done) | copy-start | bytes 1179652
  121.5 6.9 %collective-permute-start.1 = (bf16[8,1536]{1,0:T(8,128)(2,1)S(1)}, bf16[8,1536]{1,0:T(8,128)(2,1)S(1)}, u32[]{:S(2)}, u32[]{:S(2)}) collective-permute-start(bf16[8,1536]{1,0:T(8,128)(2,1)S(1)} %get-tuple-element.10), channel_id=1, source_target_pairs={{0,8},{8,16},{16,24},{24,32},{32,40},{40,48},{48,56},{1,9},{9,17},... | collective-permute-start | bytes 73736 | tf_op jit(solution)/shard_map/ppermute | solution.py:345
  123.4 5.1 %collective-permute-start.2 = (bf16[8,1536]{1,0:T(8,128)(2,1)S(1)}, bf16[8,1536]{1,0:T(8,128)(2,1)S(1)}, u32[]{:S(2)}, u32[]{:S(2)}) collective-permute-start(bf16[8,1536]{1,0:T(8,128)(2,1)S(1)} %get-tuple-element.11), channel_id=1, source_target_pairs={{8,0},{16,8},{24,16},{32,24},{40,32},{48,40},{56,48},{9,1},{17,9},... | collective-permute-start | bytes 73736 | tf_op jit(solution)/shard_map/ppermute | solution.py:347
  139.9 1.6 copy-start
  139.9 1.7 copy-start.1
Sparse Core Ops, SparseCore 0:
  10.1 71.7 all-gather.2
  86.8 33.8 reduce-scatter.1

commit v2 on v1

--- a/solution.py
+++ b/solution.py
@@ -1,5 +1,3 @@
-import functools
-
 import jax
 import jax.numpy as jnp
 from jax import lax
@@ -10,6 +8,8 @@
 MESH = pl.DeviceIdType.MESH
 NT = (((1,), (1,)), ((), ()))
 CHUNKS = 6
+HALO = 16
+LANES = 128
 RING = 4
 F32 = jnp.float32
 BF16 = jnp.bfloat16
@@ -66,13 +66,15 @@
     pltpu.make_async_copy(ref, ref, sem).wait()
 
 
-def tail_kernel(
-    gp, xg, w, gx, dw,
-    G, XT, D, xrel, xrec, S, zrel, zrec, rr, rl, part,
-    sends, col_send, g_recv, xrel_sem, xrec_sem, zrel_sem, zrec_sem, out_sem, rr_sem, rl_sem,
+def whole_kernel(
+    tile, w, ft, it, go, gx, dw,
+    XG, XT, acc, psend, pair, Dy, yrel, yrec, win, goa,
+    G, D, xrel, xrec, S, zrel, zrec, rr, rl, part,
+    sends, ag_send, ag_recv, p_send, p_recv, y_send, yrel_sem, yrec_sem, h_send, h_recv,
+    col_send, g_recv, xrel_sem, xrec_sem, zrel_sem, zrec_sem, out_sem, rr_sem, rl_sem,
 ):
     me = Place()
-    rows = gp.shape[0]
+    rows = tile.shape[0]
     half = rows // 2
     wide = w.shape[2]
     step = 3 * wide // CHUNKS
@@ -82,14 +84,265 @@
     xr, xl = me.at_x(1), me.at_x(-1)
     up, down = me.at_z(4), me.at_z(-4)
     col_up, col_down = me.at_col(1), me.at_col(-1)
-    greet([right, left, sibling, xr, xl, up, down, col_up, col_down])
+    far = (me.dp, (me.row + 2 * me.core + 7) % 8, me.col)
+    greet([right, left, sibling, far, xr, xl, up, down, col_up, col_down])
     out = Sends(sends)
+    top, bottom = pl.ds(0, half), pl.ds(half, half)
+    halves = (top, bottom)
+
+    before, after = (me.dp, (me.row + 7) % 8, me.col), (me.dp, (me.row + 1) % 8, me.col)
+
+    def halo_copy(n):
+        src, dst, device = (
+            (go.at[pl.ds(0, HALO)], goa, before),
+            (win.at[pl.ds(HALO, HALO)], win.at[pl.ds(rows + HALO, HALO)], before),
+            (win.at[pl.ds(rows, HALO)], win.at[pl.ds(0, HALO)], after),
+        )[n]
+        return pltpu.make_async_remote_copy(
+            src_ref=src, dst_ref=dst, send_sem=h_send.at[n], recv_sem=h_recv.at[n],
+            device_id=device, device_id_type=MESH,
+        )
+
+    @pl.when(me.row > 0)
+    def _():
+        halo_copy(0).start()
+
+    @pl.when(me.row == 0)
+    def _():
+        win[0:HALO, :] = jnp.zeros((HALO, 3 * wide), BF16)
+
+    @pl.when(me.row == 7)
+    def _():
+        win[rows + HALO :, :] = jnp.zeros((HALO, 3 * wide), BF16)
+        goa[...] = jnp.zeros_like(goa)
+
+    def block_at(j):
+        return pl.ds(pl.multiple_of(j * rows, rows), rows)
+
+    def line_copy(j, device):
+        return pltpu.make_async_remote_copy(
+            src_ref=XG.at[block_at(j)], dst_ref=XG.at[block_at(j)], send_sem=ag_send.at[j],
+            recv_sem=ag_recv.at[j], device_id=device, device_id_type=MESH,
+        )
+
+    def own_copy(n):
+        return pltpu.make_async_remote_copy(
+            src_ref=tile, dst_ref=XG.at[block_at(me.col)],
+            send_sem=ag_send.at[8] if n else ag_send.at[me.col],
+            recv_sem=ag_recv.at[me.col], device_id=col_down if n else col_up, device_id_type=MESH,
+        )
+
+    @pl.when(me.col < 7)
+    def _():
+        own_copy(0).start()
+
+    @pl.when(me.col > 0)
+    def _():
+        own_copy(1).start()
+
+    XG[block_at(me.col), :] = tile[...]
+
+    def pair_copy(p):
+        return pltpu.make_async_remote_copy(
+            src_ref=psend.at[p], dst_ref=pair.at[p], send_sem=p_send.at[p], recv_sem=p_recv.at[p],
+            device_id=sibling, device_id_type=MESH,
+        )
+
+    def project(j):
+        x = XG[block_at(j), :]
+        p = j // 2
+        mine = j % 2 == me.core
+        for c in range(3):
+            at = slice(c * wide, (c + 1) * wide)
+            product = jnp.dot(x, w[c], preferred_element_type=F32)
+
+            @pl.when(mine)
+            def _():
+                acc[p, :, at] = product
+
+            @pl.when(jnp.logical_not(mine))
+            def _():
+                psend[p, :, at] = product.astype(BF16)
+
+        @pl.when(jnp.logical_not(mine))
+        def _():
+            pair_copy(p).start()
+
+        XT[:, block_at(j)] = x.T
+
+    y_opp, y_r, y_l = ((me.y + by) % RING for by in (2, 1, 3))
+
+    def y_copy(n):
+        src, dst, sem, device = (
+            (Dy.at[y_opp, top], yrel.at[0], yrel_sem.at[0], right),
+            (Dy.at[y_opp, bottom], yrel.at[1], yrel_sem.at[1], left),
+            (Dy.at[y_r, bottom], yrec.at[0, bottom], yrec_sem.at[0, 1], right),
+            (Dy.at[y_l, top], yrec.at[1, top], yrec_sem.at[1, 0], left),
+            (Dy.at[y_r, top], yrec.at[0, top], yrec_sem.at[0, 0], right),
+            (Dy.at[y_l, bottom], yrec.at[1, bottom], yrec_sem.at[1, 1], left),
+        )[n]
+        return pltpu.make_async_remote_copy(
+            src_ref=src, dst_ref=dst, send_sem=y_send.at[n], recv_sem=sem, device_id=device,
+            device_id_type=MESH,
+        )
+
+    def piece(d):
+        sign = (2 * (d % 2) - 1) * (1 - 2 * (me.col % 2))
+        p = me.col // 2 + sign * (d // 2)
+        return p, jnp.logical_and(jnp.logical_and(p >= 0, p < RING), jnp.logical_and(d >= 1, d <= 7))
+
+    def pair_sum(d):
+        p, there = piece(d)
+        role = (p - me.y + RING) % RING
+
+        @pl.when(there)
+        def _():
+            arrived(pair.at[p], p_recv.at[p], me)
+
+        @pl.when(jnp.logical_and(there, role == 0))
+        def _():
+            acc[p] = acc[p] + pair[p].astype(F32)
+
+        @pl.when(jnp.logical_and(there, role != 0))
+        def _():
+            Dy[p] = (acc[p] + pair[p].astype(F32)).astype(BF16)
+
+        @pl.when(jnp.logical_and(there, role == 2))
+        def _():
+            y_copy(0).start()
+            y_copy(1).start()
+
+        @pl.when(jnp.logical_and(there, role == 1))
+        def _():
+            y_copy(2).start()
+
+        @pl.when(jnp.logical_and(there, role == 3))
+        def _():
+            y_copy(3).start()
+
+    def relay_y(d):
+        p, there = piece(d)
+        role = (p - me.y + RING) % RING
+
+        @pl.when(jnp.logical_and(there, role == 1))
+        def _():
+            arrived(yrel.at[0], yrel_sem.at[0], me)
+            Dy[p, top] = (Dy[p, top].astype(F32) + yrel[0].astype(F32)).astype(BF16)
+            y_copy(4).start()
+
+        @pl.when(jnp.logical_and(there, role == 3))
+        def _():
+            arrived(yrel.at[1], yrel_sem.at[1], me)
+            Dy[p, bottom] = (Dy[p, bottom].astype(F32) + yrel[1].astype(F32)).astype(BF16)
+            y_copy(5).start()
+
+    project(me.col)
+
+    def line_step(d, carry):
+        from_below = jnp.logical_and(d <= 7, me.col - d >= 0)
+        from_above = jnp.logical_and(d <= 7, me.col + d <= 7)
+
+        @pl.when(from_below)
+        def _():
+            j = me.col - d
+            arrived(XG.at[block_at(j)], ag_recv.at[j], me)
+
+            @pl.when(me.col < 7)
+            def _():
+                line_copy(j, col_up).start()
+
+        @pl.when(from_above)
+        def _():
+            j = me.col + d
+            arrived(XG.at[block_at(j)], ag_recv.at[j], me)
+
+            @pl.when(me.col > 0)
+            def _():
+                line_copy(j, col_down).start()
+
+        @pl.when(from_below)
+        def _():
+            project(me.col - d)
+
+        @pl.when(from_above)
+        def _():
+            project(me.col + d)
+
+        relay_y(d - 2)
+        pair_sum(d - 1)
+        return carry
+
+    lax.fori_loop(1, 10, line_step, 0)
+
+    for side in range(2):
+        for h in range(2):
+            arrived(yrec.at[side, halves[h]], yrec_sem.at[side, h], me)
+    win[HALO : rows + HALO, :] = (acc[me.y] + yrec[0].astype(F32) + yrec[1].astype(F32)).astype(BF16)
+
+    @pl.when(me.row > 0)
+    def _():
+        halo_copy(1).start()
+
+    @pl.when(me.row < 7)
+    def _():
+        halo_copy(2).start()
+
+    @pl.when(me.row > 0)
+    def _():
+        arrived(win.at[pl.ds(0, HALO)], h_recv.at[2], me)
+
+    @pl.when(me.row < 7)
+    def _():
+        arrived(win.at[pl.ds(rows + HALO, HALO)], h_recv.at[1], me)
+        arrived(goa, h_recv.at[0], me)
+
+    length = rows + 2 * HALO
+
+    def causal(seq, taps):
+        total = taps[0] * seq
+        for lag in range(1, len(taps)):
+            total = total + taps[lag] * pltpu.roll(seq, lag, 0)
+        return total
+
+    def anticausal(seq, taps):
+        total = taps[0] * seq
+        for lag in range(1, len(taps)):
+            total = total + taps[lag] * pltpu.roll(seq, length - lag, 0)
+        return total
+
+    mine = block_at(me.row)
+
+    def channels(n, carry):
+        def at(c):
+            return pl.ds(pl.multiple_of(c * wide + n * LANES, LANES), LANES)
+
+        taps = [[ft[s, c : c + 1, at(0)] for s in range(3)] for c in range(3)]
+        inner_taps = [it[s : s + 1, at(0)] for s in range(7)]
+        query, key, value = (causal(win[:, at(c)].astype(F32), taps[c]) for c in range(3))
+        upstream = jnp.concatenate(
+            [
+                jnp.zeros((HALO, LANES), F32),
+                go[:, at(0)].astype(F32),
+                goa[:, at(0)].astype(F32),
+            ],
+            axis=0,
+        )
+        product = (key * value).astype(BF16).astype(F32)
+        inner = causal(product, inner_taps)
+        grad_product = anticausal(upstream * query, inner_taps)
+        mixed = (upstream * inner, grad_product * value, grad_product * key)
+        for c in range(3):
+            grad = anticausal(mixed[c], taps[c])
+            G[mine, at(c)] = grad[HALO : rows + HALO].astype(BF16)
+        return carry
+
+    lax.fori_loop(0, wide // LANES, channels, 0)
 
     def g_at(slot, h):
         return G.at[pl.ds(pl.multiple_of(slot * rows + h * half, half), half)]
 
-    def g_send(src, slot, h, device):
-        out.start(src, g_at(slot, h), g_recv.at[slot, h], device)
+    def g_send(slot, h, device):
+        out.start(g_at(slot, h), g_at(slot, h), g_recv.at[slot, h], device)
 
     def g_wait(slot, h):
         arrived(g_at(slot, h), g_recv.at[slot, h], me)
@@ -100,16 +353,12 @@
     def other(by):
         return ((me.y + by + RING) % RING) * 2 + 1 - me.core
 
-    own = [gp.at[pl.ds(h * half, half)] for h in range(2)]
-    g_send(own[0], me.row, 0, right)
-    g_send(own[1], me.row, 1, left)
-    g_send(own[1], me.row, 1, right)
-    g_send(own[0], me.row, 0, left)
+    g_send(me.row, 0, right)
+    g_send(me.row, 1, left)
+    g_send(me.row, 1, right)
+    g_send(me.row, 0, left)
     for h in range(2):
-        g_send(own[h], me.row, h, sibling)
-    G[pl.ds(pl.multiple_of(me.row * rows, rows), rows), :] = gp[...]
-    for b in range(8):
-        XT[:, b * rows : (b + 1) * rows] = xg[b * rows : (b + 1) * rows, :].T
+        g_send(me.row, h, sibling)
 
     @pl.when(me.col == 7)
     def _():
@@ -120,19 +369,19 @@
         rl[...] = jnp.zeros_like(rl)
 
     g_wait(same(-1), 0)
-    g_send(g_at(same(-1), 0), same(-1), 0, right)
-    g_send(g_at(same(-1), 0), same(-1), 0, sibling)
+    g_send(same(-1), 0, right)
+    g_send(same(-1), 0, sibling)
     g_wait(same(1), 1)
-    g_send(g_at(same(1), 1), same(1), 1, left)
-    g_send(g_at(same(1), 1), same(1), 1, sibling)
+    g_send(same(1), 1, left)
+    g_send(same(1), 1, sibling)
     g_wait(same(-1), 1)
-    g_send(g_at(same(-1), 1), same(-1), 1, sibling)
+    g_send(same(-1), 1, sibling)
     g_wait(same(1), 0)
-    g_send(g_at(same(1), 0), same(1), 0, sibling)
+    g_send(same(1), 0, sibling)
     g_wait(same(2), 0)
-    g_send(g_at(same(2), 0), same(2), 0, sibling)
+    g_send(same(2), 0, sibling)
     g_wait(same(2), 1)
-    g_send(g_at(same(2), 1), same(2), 1, sibling)
+    g_send(same(2), 1, sibling)
     for by in (0, -1, 1, 2):
         for h in range(2):
             g_wait(other(by), h)
@@ -199,8 +448,6 @@
             def _():
                 col_copy(block, 1).wait_send()
 
-    top, bottom = pl.ds(0, half), pl.ds(half, half)
-    halves = (top, bottom)
     to_r, to_l, to_o = ((me.x + by + RING) % RING for by in (1, 3, 2))
 
     def dw_at(q, h, m):
@@ -288,35 +535,82 @@
         stage(m)
     out.finish()
 
+    @pl.when(me.col < 7)
+    def _():
+        own_copy(0).wait_send()
+
+    @pl.when(me.col > 0)
+    def _():
+        own_copy(1).wait_send()
+
+    for j in range(8):
+
+        @pl.when(jnp.logical_and(j < me.col, me.col < 7))
+        def _():
+            line_copy(j, col_up).wait_send()
+
+        @pl.when(jnp.logical_and(j > me.col, me.col > 0))
+        def _():
+            line_copy(j, col_down).wait_send()
+
+    for p in range(RING):
+        pair_copy(p).wait_send()
+    for n in range(6):
+        y_copy(n).wait_send()
+
+    @pl.when(me.row > 0)
+    def _():
+        halo_copy(0).wait_send()
+        halo_copy(1).wait_send()
+
+    @pl.when(me.row < 7)
+    def _():
+        halo_copy(2).wait_send()
+
 
 SENDS = 6 + 8 + CHUNKS * (4 + 2 + 2 + 2 + 4 + 2)
 
 
-def tail(gp, xg, w):
-    rows, wide = gp.shape[0], w.shape[2]
+def whole(tile, w, ft, it, go):
+    rows, wide, deep = tile.shape[0], w.shape[2], w.shape[1]
     half, step = rows // 2, 3 * wide // CHUNKS
     vmem, sem = pltpu.VMEM, pltpu.SemaphoreType.DMA
     return pl.pallas_call(
-        tail_kernel,
-        out_shape=(
-            jax.ShapeDtypeStruct((rows, w.shape[1]), BF16),
-            jax.ShapeDtypeStruct(w.shape, BF16),
-        ),
-        in_specs=[pl.BlockSpec(memory_space=pltpu.VMEM)] * 3,
+        whole_kernel,
+        out_shape=(jax.ShapeDtypeStruct((rows, deep), BF16), jax.ShapeDtypeStruct(w.shape, BF16)),
+        in_specs=[pl.BlockSpec(memory_space=pltpu.VMEM)] * 5,
         out_specs=(pl.BlockSpec(memory_space=pltpu.VMEM),) * 2,
         scratch_shapes=[
+            vmem((8 * rows, deep), BF16),
+            vmem((deep, 8 * rows), BF16),
+            vmem((RING, rows, 3 * wide), F32),
+            vmem((RING, rows, 3 * wide), BF16),
+            vmem((RING, rows, 3 * wide), BF16),
+            vmem((RING, rows, 3 * wide), BF16),
+            vmem((2, half, 3 * wide), BF16),
+            vmem((2, rows, 3 * wide), BF16),
+            vmem((rows + 2 * HALO, 3 * wide), BF16),
+            vmem((HALO, wide), BF16),
             vmem((8 * rows, 3 * wide), BF16),
-            vmem((w.shape[1], 8 * rows), BF16),
             vmem((RING, CHUNKS, rows, step), BF16),
             vmem((2, CHUNKS, half, step), BF16),
             vmem((2, CHUNKS, rows, step), BF16),
             vmem((CHUNKS, rows, step), BF16),
             vmem((2, CHUNKS, half, step), BF16),
             vmem((CHUNKS, rows, step), BF16),
-            vmem((8, rows, w.shape[1]), BF16),
-            vmem((8, rows, w.shape[1]), BF16),
-            vmem((8, rows, w.shape[1]), BF16),
+            vmem((8, rows, deep), BF16),
+            vmem((8, rows, deep), BF16),
+            vmem((8, rows, deep), BF16),
             sem((SENDS,)),
+            sem((9,)),
+            sem((8,)),
+            sem((RING,)),
+            sem((RING,)),
+            sem((6,)),
+            sem((2,)),
+            sem((2, 2)),
+            sem((3,)),
+            sem((3,)),
             sem((8,)),
             sem((8, 2)),
             sem((2, CHUNKS)),
@@ -328,100 +622,17 @@
             sem((8,)),
         ],
         compiler_params=pltpu.CompilerParams(
-            collective_id=1, has_side_effects=True, vmem_limit_bytes=44 * 2**20
+            collective_id=1, has_side_effects=True, vmem_limit_bytes=50 * 2**20
         ),
-        name="tail",
-    )(gp, xg, w)
-
-
-def with_halo(cells, sides, width):
-    for axis, dim in sides:
-        count = lax.axis_size(axis)
-        ends = count - 1
-        head = lax.slice_in_dim(cells, 0, width, axis=dim)
-        tail = lax.slice_in_dim(cells, cells.shape[dim] - width, cells.shape[dim], axis=dim)
-        cells = jnp.concatenate(
-            [
-                lax.ppermute(tail, axis, [(i, (i + 1) % count) for i in range(ends)]),
-                cells,
-                lax.ppermute(head, axis, [((i + 1) % count, i) for i in range(ends)]),
-            ],
-            axis=dim,
-        )
-    return cells
-
-
-def shifted(shard, axis, by):
-    length = lax.axis_size(axis)
-    pairs = [(i, i + by) for i in range(length) if 0 <= i + by < length]
-    return lax.ppermute(shard, axis, pairs)
-
-
-def causal(seq, taps):
-    total = taps[0] * seq
-    for lag in range(1, taps.shape[0]):
-        pad = jnp.zeros((lag,) + seq.shape[1:], jnp.float32)
-        total = total + taps[lag] * jnp.concatenate([pad, seq[:-lag]], axis=0)
-    return total
-
-
-def anticausal(seq, taps):
-    total = taps[0] * seq
-    for lag in range(1, taps.shape[0]):
-        pad = jnp.zeros((lag,) + seq.shape[1:], jnp.float32)
-        total = total + taps[lag] * jnp.concatenate([seq[lag:], pad], axis=0)
-    return total
-
-
-def rounded(value):
-    return lax.optimization_barrier(value.astype(jnp.bfloat16)).astype(jnp.float32)
+        name="whole",
+    )(tile, w, ft, it, go)
 
 
 def on_device(inputs, weights, feature_taps, inner_taps, grad_out):
-    tile = inputs[0]
-    upstream_tile = grad_out[0]
-    rows_dev = upstream_tile.shape[0]
-    width_row = weights.shape[0]
-    width_col = weights.shape[2]
-    margin = feature_taps.shape[0] - 1 + (inner_taps.shape[0] - 1)
-    flat_w = weights.reshape(width_row, 3 * width_col)
-    columns = lax.all_gather(tile, "col", axis=0, tiled=True)
-    block = columns
-    proj = lax.psum_scatter(
-        jnp.dot(block, flat_w, preferred_element_type=jnp.float32).astype(jnp.bfloat16),
-        "row",
-        scatter_dimension=0,
-        tiled=True,
+    grad_x, grad_w = whole(
+        inputs[0], weights.transpose(1, 0, 2), feature_taps, inner_taps, grad_out[0]
     )
-    padded = with_halo(proj, (("row", 0),), margin)
-    after = shifted(upstream_tile[:margin], "row", -1)
-    length = rows_dev + 2 * margin
-    window = padded.astype(jnp.float32).reshape(length, 3, width_col)
-    upstream = jnp.concatenate(
-        [
-            jnp.zeros((margin, width_col), jnp.float32),
-            upstream_tile.astype(jnp.float32),
-            after.astype(jnp.float32),
-        ],
-        axis=0,
-    )
-    mixed = causal(window, feature_taps)
-    query = mixed[:, 0]
-    key = mixed[:, 1]
-    value = mixed[:, 2]
-    product = rounded(key * value)
-    inner = causal(product, inner_taps)
-    grad_query = upstream * inner
-    grad_inner = upstream * query
-    grad_product = anticausal(grad_inner, inner_taps)
-    grad_mixed = jnp.stack([grad_query, grad_product * value, grad_product * key], axis=1)
-    grad_proj = anticausal(grad_mixed, feature_taps)[margin : margin + rows_dev].astype(
-        jnp.bfloat16
-    )
-    grad_x, grad_w = tail(
-        grad_proj.reshape(rows_dev, 3 * width_col), columns, weights.transpose(1, 0, 2)
-    )
-    return grad_x[None], grad_w.astype(jnp.float32).transpose(1, 0, 2)
+    return grad_x[None], grad_w.astype(F32).transpose(1, 0, 2)
 
 
 def solution(mesh):

time: 260 us -> 172 us (0.66)
  the two profiles are of different devices: /device:TPU:8 before, /device:TPU:2 now
where the time goes in v2:
time: 172 us
  Pallas kernels  163 us (95%)
  local copies, waits for them, and re-layouts  5.32 us (3%)
  other arithmetic  2.11 us (1%)
    pallas_call x1, Pallas kernels, whole(): pl.pallas_call(whole_kernel, out_shape=(jax.ShapeDtypeStruct((rows, deep)...  163 us
    unnamed x11, local copies, waits for them, and re-layouts  5.32 us

profile of v2, /device:TPU:2, one launch (start us, length us, event | category | flops | bytes accessed | tf_op | source)
XLA Modules:
  0.0 171.5 jit_solution(15149207806959208542)
XLA Ops:
  0.6 0.0 copy-start
  0.6 1.4 copy-done
  2.0 0.0 copy-start.1
  2.0 0.9 copy-done.1
  2.9 0.0 copy-start.2
  2.9 0.9 copy-done.2
  3.8 0.0 copy-start.3
  3.9 0.7 copy-done.3
  4.6 0.0 copy-start.4
  4.6 0.7 copy-done.4
  5.3 163.4 %whole.1 = (bf16[128,512]{1,0:T(8,128)(2,1)S(1)}, bf16[3,512,512]{2,1,0:T(8,128)(2,1)S(1)}) custom-call(bf16[128,512]{1,0:T(8,128)(2,1)S(1)} %bitcast.7, bf16[3,512,512]{2,1,0:T(8,128)(2,1)S(1)} %bitcast.6, f32[3,3,512]{2,1,0:T(4,128)S(1)} %copy-done.3, f32[7,512]{1,0:T(8,128)S(1)} %copy-done.4, bf16[128,512]{1,0:T(8,128)(2,1)S(1)} %bitcast.8), custom_call_target="tpu_custom_call" | custom-call | tf_op jit(solution)/shard_map/whole/pallas_call | solution.py:578
  168.8 2.1 %convert_bitcast_fusion = f32[512,3,512]{2,0,1:T(8,128)} fusion(bf16[3,512,512]{2,1,0:T(8,128)(2,1)S(1)} %get-tuple-element.5), kind=kLoop, calls=%fused_computation | loop fusion | flops 786432 | bytes 4718592 | tf_op jit(solution)/shard_map/transpose | solution.py:635
  170.9 0.7 copy.8
Async XLA Ops:
  0.6 1.4 copy-start
  2.0 0.9 copy-start.1
  2.9 0.9 copy-start.2
  3.8 0.7 copy-start.3
  4.6 0.7 copy-start.4

commit v3 on v2

--- a/solution.py
+++ b/solution.py
@@ -10,7 +10,14 @@
 CHUNKS = 6
 HALO = 16
 LANES = 128
+SUBS = 4
 RING = 4
+ORDER = (
+    "M0 M1 C0 X0", "M2 E0 X1 M3", "E1 C1 X2 M4", "E2 X3 M5 E3",
+    "C2 X4 E4 X5", "E5 C3 Z0 Z1", "Z2 Z3 Z4 Z5", "C4 T0 T1 O0",
+    "C5 T2 O1 T3", "O2 L0 C6 T4", "O3 L1 G0 T5", "O4 L2 L3 O5",
+    "L4 L5",
+)
 F32 = jnp.float32
 BF16 = jnp.bfloat16
 
@@ -67,10 +74,10 @@
 
 
 def whole_kernel(
-    tile, w, ft, it, go, gx, dw,
-    XG, XT, acc, psend, pair, Dy, yrel, yrec, win, goa,
+    tile, w_hbm, ft, it, go_hbm, gx, dw,
+    w, go, XG, XT, acc, psend, pair, Dy, yrel, yrec, win, goa,
     G, D, xrel, xrec, S, zrel, zrec, rr, rl, part,
-    sends, ag_send, ag_recv, p_send, p_recv, y_send, yrel_sem, yrec_sem, h_send, h_recv,
+    fetch_sem, sends, ag_send, ag_recv, p_send, p_recv, y_send, yrel_sem, yrec_sem, h_send, h_recv,
     col_send, g_recv, xrel_sem, xrec_sem, zrel_sem, zrec_sem, out_sem, rr_sem, rl_sem,
 ):
     me = Place()
@@ -85,6 +92,14 @@
     up, down = me.at_z(4), me.at_z(-4)
     col_up, col_down = me.at_col(1), me.at_col(-1)
     far = (me.dp, (me.row + 2 * me.core + 7) % 8, me.col)
+    own_rows = pl.ds(pl.multiple_of(me.col * rows, rows), rows)
+    fetches = [
+        pltpu.make_async_copy(tile, XG.at[own_rows], fetch_sem.at[0]),
+        pltpu.make_async_copy(w_hbm, w, fetch_sem.at[1]),
+        pltpu.make_async_copy(go_hbm, go, fetch_sem.at[2]),
+    ]
+    for copy in fetches:
+        copy.start()
     greet([right, left, sibling, far, xr, xl, up, down, col_up, col_down])
     out = Sends(sends)
     top, bottom = pl.ds(0, half), pl.ds(half, half)
@@ -94,7 +109,7 @@
 
     def halo_copy(n):
         src, dst, device = (
-            (go.at[pl.ds(0, HALO)], goa, before),
+            (go_hbm.at[pl.ds(0, HALO)], goa, before),
             (win.at[pl.ds(HALO, HALO)], win.at[pl.ds(rows + HALO, HALO)], before),
             (win.at[pl.ds(rows, HALO)], win.at[pl.ds(0, HALO)], after),
         )[n]
@@ -119,28 +134,37 @@
     def block_at(j):
         return pl.ds(pl.multiple_of(j * rows, rows), rows)
 
-    def line_copy(j, device):
+    def sub_at(j, u):
+        sub = rows // SUBS
+        return pl.ds(pl.multiple_of(j * rows + u * sub, sub), sub)
+
+    def line_copy(j, u, device):
         return pltpu.make_async_remote_copy(
-            src_ref=XG.at[block_at(j)], dst_ref=XG.at[block_at(j)], send_sem=ag_send.at[j],
-            recv_sem=ag_recv.at[j], device_id=device, device_id_type=MESH,
-        )
-
-    def own_copy(n):
+            src_ref=XG.at[sub_at(j, u)], dst_ref=XG.at[sub_at(j, u)], send_sem=ag_send.at[j, u],
+            recv_sem=ag_recv.at[j, u], device_id=device, device_id_type=MESH,
+        )
+
+    def own_copy(n, u):
+        sub = rows // SUBS
         return pltpu.make_async_remote_copy(
-            src_ref=tile, dst_ref=XG.at[block_at(me.col)],
-            send_sem=ag_send.at[8] if n else ag_send.at[me.col],
-            recv_sem=ag_recv.at[me.col], device_id=col_down if n else col_up, device_id_type=MESH,
+            src_ref=tile.at[pl.ds(u * sub, sub)], dst_ref=XG.at[sub_at(me.col, u)],
+            send_sem=ag_send.at[8, u] if n else ag_send.at[me.col, u],
+            recv_sem=ag_recv.at[me.col, u], device_id=col_down if n else col_up,
+            device_id_type=MESH,
         )
 
     @pl.when(me.col < 7)
     def _():
-        own_copy(0).start()
+        for u in range(SUBS):
+            own_copy(0, u).start()
 
     @pl.when(me.col > 0)
     def _():
-        own_copy(1).start()
-
-    XG[block_at(me.col), :] = tile[...]
+        for u in range(SUBS):
+            own_copy(1, u).start()
+
+    for copy in fetches:
+        copy.wait()
 
     def pair_copy(p):
         return pltpu.make_async_remote_copy(
@@ -236,43 +260,46 @@
             Dy[p, bottom] = (Dy[p, bottom].astype(F32) + yrel[1].astype(F32)).astype(BF16)
             y_copy(5).start()
 
-    project(me.col)
+    def pass_on(d, some):
+        @pl.when(jnp.logical_and(d <= 7, me.col - d >= 0))
+        def _():
+            j = me.col - d
+            for u in some:
+                arrived(XG.at[sub_at(j, u)], ag_recv.at[j, u], me)
+
+                @pl.when(me.col < 7)
+                def _():
+                    line_copy(j, u, col_up).start()
+
+        @pl.when(jnp.logical_and(d <= 7, me.col + d <= 7))
+        def _():
+            j = me.col + d
+            for u in some:
+                arrived(XG.at[sub_at(j, u)], ag_recv.at[j, u], me)
+
+                @pl.when(me.col > 0)
+                def _():
+                    line_copy(j, u, col_down).start()
 
     def line_step(d, carry):
-        from_below = jnp.logical_and(d <= 7, me.col - d >= 0)
-        from_above = jnp.logical_and(d <= 7, me.col + d <= 7)
-
-        @pl.when(from_below)
-        def _():
-            j = me.col - d
-            arrived(XG.at[block_at(j)], ag_recv.at[j], me)
-
-            @pl.when(me.col < 7)
-            def _():
-                line_copy(j, col_up).start()
-
-        @pl.when(from_above)
-        def _():
-            j = me.col + d
-            arrived(XG.at[block_at(j)], ag_recv.at[j], me)
-
-            @pl.when(me.col > 0)
-            def _():
-                line_copy(j, col_down).start()
-
-        @pl.when(from_below)
-        def _():
-            project(me.col - d)
-
-        @pl.when(from_above)
-        def _():
-            project(me.col + d)
-
-        relay_y(d - 2)
-        pair_sum(d - 1)
+        last = d - 1
+        pass_on(d, range(SUBS // 2))
+
+        @pl.when(jnp.logical_and(last <= 7, me.col - last >= 0))
+        def _():
+            project(me.col - last)
+
+        pass_on(d, range(SUBS // 2, SUBS))
+
+        @pl.when(jnp.logical_and(jnp.logical_and(last >= 1, last <= 7), me.col + last <= 7))
+        def _():
+            project(me.col + last)
+
+        relay_y(d - 3)
+        pair_sum(d - 2)
         return carry
 
-    lax.fori_loop(1, 10, line_step, 0)
+    lax.fori_loop(1, 11, line_step, 0)
 
     for side in range(2):
         for h in range(2):
@@ -395,58 +422,60 @@
             )
         return total
 
-    def col_copy(block, side):
+    def col_copy(block, side, h):
         landing, sems, device = ((rr, rr_sem, col_down), (rl, rl_sem, col_up))[side]
         return pltpu.make_async_remote_copy(
-            src_ref=part.at[block], dst_ref=landing.at[block], send_sem=col_send.at[block],
-            recv_sem=sems.at[block], device_id=device, device_id_type=MESH,
-        )
+            src_ref=part.at[block, halves[h]], dst_ref=landing.at[block, halves[h]],
+            send_sem=col_send.at[block, h], recv_sem=sems.at[block, h], device_id=device,
+            device_id_type=MESH,
+        )
+
+    def col_pass(block, side, inner):
+        landing, sems = ((rr, rr_sem), (rl, rl_sem))[side]
+        total = grad_in_of(block)
+        for h in range(2):
+
+            @pl.when(inner)
+            def _():
+                arrived(landing.at[block, halves[h]], sems.at[block, h], me)
+
+            own = total[h * half : (h + 1) * half]
+            part[block, halves[h]] = (own + landing[block, halves[h]].astype(F32)).astype(BF16)
+            col_copy(block, side, h).start()
 
     def col_round(s):
         @pl.when(s + me.col >= 7)
         def _():
-            block = s + me.col - 7
+            col_pass(s + me.col - 7, 0, me.col < 7)
+
+        @pl.when(s >= me.col)
+        def _():
+            col_pass(7 - s + me.col, 1, me.col > 0)
+
+    def col_last(unused):
+        total = grad_in_of(me.col)
+        for h in range(2):
 
             @pl.when(me.col < 7)
             def _():
-                arrived(rr.at[block], rr_sem.at[block], me)
-
-            part[block] = (grad_in_of(block) + rr[block].astype(F32)).astype(BF16)
-            col_copy(block, 0).start()
-
-        @pl.when(s >= me.col)
-        def _():
-            block = 7 - s + me.col
+                arrived(rr.at[me.col, halves[h]], rr_sem.at[me.col, h], me)
 
             @pl.when(me.col > 0)
             def _():
-                arrived(rl.at[block], rl_sem.at[block], me)
-
-            part[block] = (grad_in_of(block) + rl[block].astype(F32)).astype(BF16)
-            col_copy(block, 1).start()
-
-    def col_last():
-        total = grad_in_of(me.col)
-
-        @pl.when(me.col < 7)
-        def _():
-            arrived(rr.at[me.col], rr_sem.at[me.col], me)
-
-        @pl.when(me.col > 0)
-        def _():
-            arrived(rl.at[me.col], rl_sem.at[me.col], me)
+                arrived(rl.at[me.col, halves[h]], rl_sem.at[me.col, h], me)
 
         gx[...] = (total + rr[me.col].astype(F32) + rl[me.col].astype(F32)).astype(BF16)
 
         for block in range(8):
-
-            @pl.when(block < me.col)
-            def _():
-                col_copy(block, 0).wait_send()
-
-            @pl.when(block > me.col)
-            def _():
-                col_copy(block, 1).wait_send()
+            for h in range(2):
+
+                @pl.when(block < me.col)
+                def _():
+                    col_copy(block, 0, h).wait_send()
+
+                @pl.when(block > me.col)
+                def _():
+                    col_copy(block, 1, h).wait_send()
 
     to_r, to_l, to_o = ((me.x + by + RING) % RING for by in (1, 3, 2))
 
@@ -519,39 +548,36 @@
         gathered(to_o, 0, m)
         gathered(to_o, 1, m)
 
-    stages = [multiply, relay_x, exchange, relay_z, total_of, relay_out, last_out]
-    order = []
-    lag = [0, 2, 3, 5, 7, 8, 9]
-    for slot in range(CHUNKS + lag[-1]):
-        for k in reversed(range(len(stages))):
-            m = slot - lag[k]
-            if 0 <= m < CHUNKS:
-                order.append((stages[k], m))
-        if 1 <= slot < 8:
-            order.append((col_round, slot - 1))
-        if slot == 8:
-            order.append((lambda unused: col_last(), 0))
-    for stage, m in order:
-        stage(m)
+    stages = {
+        "M": multiply, "X": relay_x, "E": exchange, "Z": relay_z, "T": total_of, "O": relay_out,
+        "L": last_out, "C": col_round, "G": col_last,
+    }
+    for group in ORDER:
+        for name in group.split():
+            stages[name[0]](int(name[1]))
     out.finish()
 
     @pl.when(me.col < 7)
     def _():
-        own_copy(0).wait_send()
+        for u in range(SUBS):
+            own_copy(0, u).wait_send()
 
     @pl.when(me.col > 0)
     def _():
-        own_copy(1).wait_send()
+        for u in range(SUBS):
+            own_copy(1, u).wait_send()
 
     for j in range(8):
 
         @pl.when(jnp.logical_and(j < me.col, me.col < 7))
         def _():
-            line_copy(j, col_up).wait_send()
+            for u in range(SUBS):
+                line_copy(j, u, col_up).wait_send()
 
         @pl.when(jnp.logical_and(j > me.col, me.col > 0))
         def _():
-            line_copy(j, col_down).wait_send()
+            for u in range(SUBS):
+                line_copy(j, u, col_down).wait_send()
 
     for p in range(RING):
         pair_copy(p).wait_send()
@@ -578,9 +604,13 @@
     return pl.pallas_call(
         whole_kernel,
         out_shape=(jax.ShapeDtypeStruct((rows, deep), BF16), jax.ShapeDtypeStruct(w.shape, BF16)),
-        in_specs=[pl.BlockSpec(memory_space=pltpu.VMEM)] * 5,
+        in_specs=[
+            pl.BlockSpec(memory_space=space) for space in (pl.ANY, pl.ANY, vmem, vmem, pl.ANY)
+        ],
         out_specs=(pl.BlockSpec(memory_space=pltpu.VMEM),) * 2,
         scratch_shapes=[
+            vmem(w.shape, BF16),
+            vmem((rows, wide), BF16),
             vmem((8 * rows, deep), BF16),
             vmem((deep, 8 * rows), BF16),
             vmem((RING, rows, 3 * wide), F32),
@@ -601,9 +631,10 @@
             vmem((8, rows, deep), BF16),
             vmem((8, rows, deep), BF16),
             vmem((8, rows, deep), BF16),
+            sem((3,)),
             sem((SENDS,)),
-            sem((9,)),
-            sem((8,)),
+            sem((9, SUBS)),
+            sem((8, SUBS)),
             sem((RING,)),
             sem((RING,)),
             sem((6,)),
@@ -611,15 +642,15 @@
             sem((2, 2)),
             sem((3,)),
             sem((3,)),
-            sem((8,)),
+            sem((8, 2)),
             sem((8, 2)),
             sem((2, CHUNKS)),
             sem((2, 2, CHUNKS)),
             sem((2, CHUNKS)),
             sem((2, CHUNKS)),
             sem((RING, 2, CHUNKS)),
-            sem((8,)),
-            sem((8,)),
+            sem((8, 2)),
+            sem((8, 2)),
         ],
         compiler_params=pltpu.CompilerParams(
             collective_id=1, has_side_effects=True, vmem_limit_bytes=50 * 2**20

time: 172 us -> 161 us (0.936)
  the two profiles are of different devices: /device:TPU:2 before, /device:TPU:32 now
where the time goes in v3:
time: 161 us
  Pallas kernels  153 us (95%)
  local copies, waits for them, and re-layouts  5.32 us (3%)
  other arithmetic  2.11 us (1%)
    pallas_call x1, Pallas kernels, whole(): pl.pallas_call(whole_kernel, out_shape=(jax.ShapeDtypeStruct((rows, deep)...  153 us
    unnamed x11, local copies, waits for them, and re-layouts  5.32 us

profile of v3, /device:TPU:32, one launch (start us, length us, event | category | flops | bytes accessed | tf_op | source)
XLA Modules:
  0.0 161.2 jit_solution(13053933422228651536)
XLA Ops:
  0.6 0.0 copy-start
  0.6 1.4 copy-done
  2.0 0.0 copy-start.1
  2.0 0.9 copy-done.1
  2.9 0.0 copy-start.2
  2.9 0.9 copy-done.2
  3.8 0.0 copy-start.3
  3.9 0.7 copy-done.3
  4.6 0.0 copy-start.4
  4.6 0.7 copy-done.4
  5.3 153.1 %whole.1 = (bf16[128,512]{1,0:T(8,128)(2,1)S(1)}, bf16[3,512,512]{2,1,0:T(8,128)(2,1)S(1)}) custom-call(bf16[128,512]{1,0:T(8,128)(2,1)S(1)} %bitcast.7, bf16[3,512,512]{2,1,0:T(8,128)(2,1)S(1)} %bitcast.6, f32[3,3,512]{2,1,0:T(4,128)S(1)} %copy-done.3, f32[7,512]{1,0:T(8,128)S(1)} %copy-done.4, bf16[128,512]{1,0:T(8,128)(2,1)S(1)} %bitcast.8), custom_call_target="tpu_custom_call" | custom-call | tf_op jit(solution)/shard_map/whole/pallas_call | solution.py:604
  158.4 2.1 %convert_bitcast_fusion = f32[512,3,512]{2,0,1:T(8,128)} fusion(bf16[3,512,512]{2,1,0:T(8,128)(2,1)S(1)} %get-tuple-element.5), kind=kLoop, calls=%fused_computation | loop fusion | flops 786432 | bytes 4718592 | tf_op jit(solution)/shard_map/transpose | solution.py:666
  160.5 0.7 copy.8
Async XLA Ops:
  0.6 1.4 copy-start
  2.0 0.9 copy-start.1
  2.9 0.9 copy-start.2
  3.8 0.7 copy-start.3
  4.6 0.7 copy-start.4

commit v4 on v3

--- a/solution.py
+++ b/solution.py
@@ -7,16 +7,16 @@
 
 MESH = pl.DeviceIdType.MESH
 NT = (((1,), (1,)), ((), ()))
-CHUNKS = 6
+CHUNKS = 4
 HALO = 16
 LANES = 128
 SUBS = 4
 RING = 4
 ORDER = (
-    "M0 M1 C0 X0", "M2 E0 X1 M3", "E1 C1 X2 M4", "E2 X3 M5 E3",
-    "C2 X4 E4 X5", "E5 C3 Z0 Z1", "Z2 Z3 Z4 Z5", "C4 T0 T1 O0",
-    "C5 T2 O1 T3", "O2 L0 C6 T4", "O3 L1 G0 T5", "O4 L2 L3 O5",
-    "L4 L5",
+    "F0 F1 H0 F2", "H1 F3 H2 A0", "H3 A1 B0 A2", "B1 W0 M0 A3",
+    "B2 W1 M1 X0", "B3 E0 W2 M2", "X1 E1 W3 M3", "X2 E2 Z0 C0",
+    "X3 E3 Z1 C1", "Z2 C2 Z3 C3", "T0 C4 O0 T1", "C5 O1 L0 T2",
+    "C6 O2 L1 T3", "G0 O3 L2 L3",
 )
 F32 = jnp.float32
 BF16 = jnp.bfloat16
@@ -74,8 +74,8 @@
 
 
 def whole_kernel(
-    tile, w_hbm, ft, it, go_hbm, gx, dw,
-    w, go, XG, XT, acc, psend, pair, Dy, yrel, yrec, win, goa,
+    tile, w_hbm, ft_hbm, it_hbm, go_hbm, gx, dw,
+    w, ft, it, go, XG, XT, acc, psend, pair, Dy, yrel, yrec, win, goa,
     G, D, xrel, xrec, S, zrel, zrec, rr, rl, part,
     fetch_sem, sends, ag_send, ag_recv, p_send, p_recv, y_send, yrel_sem, yrec_sem, h_send, h_recv,
     col_send, g_recv, xrel_sem, xrec_sem, zrel_sem, zrec_sem, out_sem, rr_sem, rl_sem,
@@ -83,9 +83,7 @@
     me = Place()
     rows = tile.shape[0]
     half = rows // 2
-    wide = w.shape[2]
-    step = 3 * wide // CHUNKS
-    per = wide // step
+    step = 3 * LANES
     right, left = me.at_y(1), me.at_y(-1)
     sibling = me.sibling()
     xr, xl = me.at_x(1), me.at_x(-1)
@@ -95,9 +93,18 @@
     own_rows = pl.ds(pl.multiple_of(me.col * rows, rows), rows)
     fetches = [
         pltpu.make_async_copy(tile, XG.at[own_rows], fetch_sem.at[0]),
-        pltpu.make_async_copy(w_hbm, w, fetch_sem.at[1]),
-        pltpu.make_async_copy(go_hbm, go, fetch_sem.at[2]),
+        pltpu.make_async_copy(go_hbm, go, fetch_sem.at[1]),
+        pltpu.make_async_copy(ft_hbm, ft, fetch_sem.at[2]),
+        pltpu.make_async_copy(it_hbm, it, fetch_sem.at[3]),
     ]
+    for n in range(CHUNKS):
+        for c in range(3):
+            lanes, to = pl.ds(n * LANES, LANES), pl.ds(c * LANES, LANES)
+            fetches.append(
+                pltpu.make_async_copy(
+                    w_hbm.at[c, :, lanes], w.at[n, :, to], fetch_sem.at[4 + 3 * n + c]
+                )
+            )
     for copy in fetches:
         copy.start()
     greet([right, left, sibling, far, xr, xl, up, down, col_up, col_down])
@@ -107,28 +114,32 @@
 
     before, after = (me.dp, (me.row + 7) % 8, me.col), (me.dp, (me.row + 1) % 8, me.col)
 
-    def halo_copy(n):
+    goa_copy = pltpu.make_async_remote_copy(
+        src_ref=go_hbm.at[pl.ds(0, HALO)], dst_ref=goa, send_sem=h_send.at[2, 0],
+        recv_sem=h_recv.at[2, 0], device_id=before, device_id_type=MESH,
+    )
+
+    def halo_copy(side, n):
         src, dst, device = (
-            (go_hbm.at[pl.ds(0, HALO)], goa, before),
-            (win.at[pl.ds(HALO, HALO)], win.at[pl.ds(rows + HALO, HALO)], before),
-            (win.at[pl.ds(rows, HALO)], win.at[pl.ds(0, HALO)], after),
-        )[n]
+            (pl.ds(HALO, HALO), pl.ds(rows + HALO, HALO), before),
+            (pl.ds(rows, HALO), pl.ds(0, HALO), after),
+        )[side]
         return pltpu.make_async_remote_copy(
-            src_ref=src, dst_ref=dst, send_sem=h_send.at[n], recv_sem=h_recv.at[n],
-            device_id=device, device_id_type=MESH,
+            src_ref=win.at[n, src], dst_ref=win.at[n, dst], send_sem=h_send.at[side, n],
+            recv_sem=h_recv.at[side, n], device_id=device, device_id_type=MESH,
         )
 
     @pl.when(me.row > 0)
     def _():
-        halo_copy(0).start()
+        goa_copy.start()
 
     @pl.when(me.row == 0)
     def _():
-        win[0:HALO, :] = jnp.zeros((HALO, 3 * wide), BF16)
+        win[:, 0:HALO, :] = jnp.zeros((CHUNKS, HALO, step), BF16)
 
     @pl.when(me.row == 7)
     def _():
-        win[rows + HALO :, :] = jnp.zeros((HALO, 3 * wide), BF16)
+        win[:, rows + HALO :, :] = jnp.zeros((CHUNKS, HALO, step), BF16)
         goa[...] = jnp.zeros_like(goa)
 
     def block_at(j):
@@ -166,47 +177,43 @@
     for copy in fetches:
         copy.wait()
 
-    def pair_copy(p):
+    def pair_copy(p, n):
         return pltpu.make_async_remote_copy(
-            src_ref=psend.at[p], dst_ref=pair.at[p], send_sem=p_send.at[p], recv_sem=p_recv.at[p],
-            device_id=sibling, device_id_type=MESH,
+            src_ref=psend.at[p, n], dst_ref=pair.at[p, n], send_sem=p_send.at[p, n],
+            recv_sem=p_recv.at[p, n], device_id=sibling, device_id_type=MESH,
         )
 
     def project(j):
         x = XG[block_at(j), :]
         p = j // 2
         mine = j % 2 == me.core
-        for c in range(3):
-            at = slice(c * wide, (c + 1) * wide)
-            product = jnp.dot(x, w[c], preferred_element_type=F32)
+        for n in range(CHUNKS):
+            product = jnp.dot(x, w[n], preferred_element_type=F32)
 
             @pl.when(mine)
             def _():
-                acc[p, :, at] = product
+                acc[p, n] = product
 
             @pl.when(jnp.logical_not(mine))
             def _():
-                psend[p, :, at] = product.astype(BF16)
-
-        @pl.when(jnp.logical_not(mine))
-        def _():
-            pair_copy(p).start()
+                psend[p, n] = product.astype(BF16)
+                pair_copy(p, n).start()
 
         XT[:, block_at(j)] = x.T
 
     y_opp, y_r, y_l = ((me.y + by) % RING for by in (2, 1, 3))
 
-    def y_copy(n):
+    def y_copy(k, n):
         src, dst, sem, device = (
-            (Dy.at[y_opp, top], yrel.at[0], yrel_sem.at[0], right),
-            (Dy.at[y_opp, bottom], yrel.at[1], yrel_sem.at[1], left),
-            (Dy.at[y_r, bottom], yrec.at[0, bottom], yrec_sem.at[0, 1], right),
-            (Dy.at[y_l, top], yrec.at[1, top], yrec_sem.at[1, 0], left),
-            (Dy.at[y_r, top], yrec.at[0, top], yrec_sem.at[0, 0], right),
-            (Dy.at[y_l, bottom], yrec.at[1, bottom], yrec_sem.at[1, 1], left),
-        )[n]
+            (Dy.at[y_opp, n, top], yrel.at[0, n], yrel_sem.at[0, n], right),
+            (Dy.at[y_opp, n, bottom], yrel.at[1, n], yrel_sem.at[1, n], left),
+            (Dy.at[y_r, n, bottom], yrec.at[0, n, bottom], yrec_sem.at[0, 1, n], right),
+            (Dy.at[y_l, n, top], yrec.at[1, n, top], yrec_sem.at[1, 0, n], left),
+            (Dy.at[y_r, n, top], yrec.at[0, n, top], yrec_sem.at[0, 0, n], right),
+            (Dy.at[y_l, n, bottom], yrec.at[1, n, bottom], yrec_sem.at[1, 1, n], left),
+        )[k]
         return pltpu.make_async_remote_copy(
-            src_ref=src, dst_ref=dst, send_sem=y_send.at[n], recv_sem=sem, device_id=device,
+            src_ref=src, dst_ref=dst, send_sem=y_send.at[k, n], recv_sem=sem, device_id=device,
             device_id_type=MESH,
         )
 
@@ -219,30 +226,32 @@
         p, there = piece(d)
         role = (p - me.y + RING) % RING
 
-        @pl.when(there)
-        def _():
-            arrived(pair.at[p], p_recv.at[p], me)
-
-        @pl.when(jnp.logical_and(there, role == 0))
-        def _():
-            acc[p] = acc[p] + pair[p].astype(F32)
-
-        @pl.when(jnp.logical_and(there, role != 0))
-        def _():
-            Dy[p] = (acc[p] + pair[p].astype(F32)).astype(BF16)
-
-        @pl.when(jnp.logical_and(there, role == 2))
-        def _():
-            y_copy(0).start()
-            y_copy(1).start()
-
-        @pl.when(jnp.logical_and(there, role == 1))
-        def _():
-            y_copy(2).start()
-
-        @pl.when(jnp.logical_and(there, role == 3))
-        def _():
-            y_copy(3).start()
+        for n in range(CHUNKS):
+
+            @pl.when(there)
+            def _():
+                arrived(pair.at[p, n], p_recv.at[p, n], me)
+
+            @pl.when(jnp.logical_and(there, role == 0))
+            def _():
+                acc[p, n] = acc[p, n] + pair[p, n].astype(F32)
+
+            @pl.when(jnp.logical_and(there, role != 0))
+            def _():
+                Dy[p, n] = (acc[p, n] + pair[p, n].astype(F32)).astype(BF16)
+
+            @pl.when(jnp.logical_and(there, role == 2))
+            def _():
+                y_copy(0, n).start()
+                y_copy(1, n).start()
+
+            @pl.when(jnp.logical_and(there, role == 1))
+            def _():
+                y_copy(2, n).start()
+
+            @pl.when(jnp.logical_and(there, role == 3))
+            def _():
+                y_copy(3, n).start()
 
     def relay_y(d):
         p, there = piece(d)
@@ -250,15 +259,19 @@
 
         @pl.when(jnp.logical_and(there, role == 1))
         def _():
-            arrived(yrel.at[0], yrel_sem.at[0], me)
-            Dy[p, top] = (Dy[p, top].astype(F32) + yrel[0].astype(F32)).astype(BF16)
-            y_copy(4).start()
+            for n in range(CHUNKS):
+                arrived(yrel.at[0, n], yrel_sem.at[0, n], me)
+                Dy[p, n, top] = (Dy[p, n, top].astype(F32) + yrel[0, n].astype(F32)).astype(BF16)
+                y_copy(4, n).start()
 
         @pl.when(jnp.logical_and(there, role == 3))
         def _():
-            arrived(yrel.at[1], yrel_sem.at[1], me)
-            Dy[p, bottom] = (Dy[p, bottom].astype(F32) + yrel[1].astype(F32)).astype(BF16)
-            y_copy(5).start()
+            for n in range(CHUNKS):
+                arrived(yrel.at[1, n], yrel_sem.at[1, n], me)
+                Dy[p, n, bottom] = (
+                    Dy[p, n, bottom].astype(F32) + yrel[1, n].astype(F32)
+                ).astype(BF16)
+                y_copy(5, n).start()
 
     def pass_on(d, some):
         @pl.when(jnp.logical_and(d <= 7, me.col - d >= 0))
@@ -301,27 +314,20 @@
 
     lax.fori_loop(1, 11, line_step, 0)
 
-    for side in range(2):
-        for h in range(2):
-            arrived(yrec.at[side, halves[h]], yrec_sem.at[side, h], me)
-    win[HALO : rows + HALO, :] = (acc[me.y] + yrec[0].astype(F32) + yrec[1].astype(F32)).astype(BF16)
-
-    @pl.when(me.row > 0)
-    def _():
-        halo_copy(1).start()
-
-    @pl.when(me.row < 7)
-    def _():
-        halo_copy(2).start()
-
-    @pl.when(me.row > 0)
-    def _():
-        arrived(win.at[pl.ds(0, HALO)], h_recv.at[2], me)
-
-    @pl.when(me.row < 7)
-    def _():
-        arrived(win.at[pl.ds(rows + HALO, HALO)], h_recv.at[1], me)
-        arrived(goa, h_recv.at[0], me)
+    def projection(n):
+        for side in range(2):
+            for h in range(2):
+                arrived(yrec.at[side, n, halves[h]], yrec_sem.at[side, h, n], me)
+        total = acc[me.y, n] + yrec[0, n].astype(F32) + yrec[1, n].astype(F32)
+        win[n, HALO : rows + HALO, :] = total.astype(BF16)
+
+        @pl.when(me.row > 0)
+        def _():
+            halo_copy(0, n).start()
+
+        @pl.when(me.row < 7)
+        def _():
+            halo_copy(1, n).start()
 
     length = rows + 2 * HALO
 
@@ -337,21 +343,27 @@
             total = total + taps[lag] * pltpu.roll(seq, length - lag, 0)
         return total
 
-    mine = block_at(me.row)
-
-    def channels(n, carry):
-        def at(c):
-            return pl.ds(pl.multiple_of(c * wide + n * LANES, LANES), LANES)
-
-        taps = [[ft[s, c : c + 1, at(0)] for s in range(3)] for c in range(3)]
-        inner_taps = [it[s : s + 1, at(0)] for s in range(7)]
-        query, key, value = (causal(win[:, at(c)].astype(F32), taps[c]) for c in range(3))
+    own_block = block_at(me.row)
+
+    def channels(n):
+        @pl.when(me.row > 0)
+        def _():
+            arrived(win.at[n, pl.ds(0, HALO)], h_recv.at[1, n], me)
+
+        @pl.when(me.row < 7)
+        def _():
+            arrived(win.at[n, pl.ds(rows + HALO, HALO)], h_recv.at[0, n], me)
+
+            if n == 0:
+                arrived(goa, h_recv.at[2, 0], me)
+
+        lanes = slice(n * LANES, (n + 1) * LANES)
+        parts = [slice(c * LANES, (c + 1) * LANES) for c in range(3)]
+        taps = [[ft[s, c : c + 1, lanes] for s in range(3)] for c in range(3)]
+        inner_taps = [it[s : s + 1, lanes] for s in range(7)]
+        query, key, value = (causal(win[n, :, parts[c]].astype(F32), taps[c]) for c in range(3))
         upstream = jnp.concatenate(
-            [
-                jnp.zeros((HALO, LANES), F32),
-                go[:, at(0)].astype(F32),
-                goa[:, at(0)].astype(F32),
-            ],
+            [jnp.zeros((HALO, LANES), F32), go[:, lanes].astype(F32), goa[:, lanes].astype(F32)],
             axis=0,
         )
         product = (key * value).astype(BF16).astype(F32)
@@ -360,19 +372,22 @@
         mixed = (upstream * inner, grad_product * value, grad_product * key)
         for c in range(3):
             grad = anticausal(mixed[c], taps[c])
-            G[mine, at(c)] = grad[HALO : rows + HALO].astype(BF16)
-        return carry
-
-    lax.fori_loop(0, wide // LANES, channels, 0)
-
-    def g_at(slot, h):
-        return G.at[pl.ds(pl.multiple_of(slot * rows + h * half, half), half)]
-
-    def g_send(slot, h, device):
-        out.start(g_at(slot, h), g_at(slot, h), g_recv.at[slot, h], device)
-
-    def g_wait(slot, h):
-        arrived(g_at(slot, h), g_recv.at[slot, h], me)
+            G[n, own_block, parts[c]] = grad[HALO : rows + HALO].astype(BF16)
+        g_send(me.row, 0, n, right)
+        g_send(me.row, 1, n, left)
+        g_send(me.row, 1, n, right)
+        g_send(me.row, 0, n, left)
+        for h in range(2):
+            g_send(me.row, h, n, sibling)
+
+    def g_at(slot, h, n):
+        return G.at[n, pl.ds(pl.multiple_of(slot * rows + h * half, half), half)]
+
+    def g_send(slot, h, n, device):
+        out.start(g_at(slot, h, n), g_at(slot, h, n), g_recv.at[slot, h, n], device)
+
+    def g_wait(slot, h, n):
+        arrived(g_at(slot, h, n), g_recv.at[slot, h, n], me)
 
     def same(by):
         return ((me.y + by + RING) % RING) * 2 + me.core
@@ -380,13 +395,6 @@
     def other(by):
         return ((me.y + by + RING) % RING) * 2 + 1 - me.core
 
-    g_send(me.row, 0, right)
-    g_send(me.row, 1, left)
-    g_send(me.row, 1, right)
-    g_send(me.row, 0, left)
-    for h in range(2):
-        g_send(me.row, h, sibling)
-
     @pl.when(me.col == 7)
     def _():
         rr[...] = jnp.zeros_like(rr)
@@ -395,31 +403,33 @@
     def _():
         rl[...] = jnp.zeros_like(rl)
 
-    g_wait(same(-1), 0)
-    g_send(same(-1), 0, right)
-    g_send(same(-1), 0, sibling)
-    g_wait(same(1), 1)
-    g_send(same(1), 1, left)
-    g_send(same(1), 1, sibling)
-    g_wait(same(-1), 1)
-    g_send(same(-1), 1, sibling)
-    g_wait(same(1), 0)
-    g_send(same(1), 0, sibling)
-    g_wait(same(2), 0)
-    g_send(same(2), 0, sibling)
-    g_wait(same(2), 1)
-    g_send(same(2), 1, sibling)
-    for by in (0, -1, 1, 2):
+    def relay_g(n):
+        g_wait(same(-1), 0, n)
+        g_send(same(-1), 0, n, right)
+        g_send(same(-1), 0, n, sibling)
+        g_wait(same(1), 1, n)
+        g_send(same(1), 1, n, left)
+        g_send(same(1), 1, n, sibling)
+        g_wait(same(-1), 1, n)
+        g_send(same(-1), 1, n, sibling)
+        g_wait(same(1), 0, n)
+        g_send(same(1), 0, n, sibling)
+
+    def share_g(n):
         for h in range(2):
-            g_wait(other(by), h)
+            g_wait(same(2), h, n)
+            g_send(same(2), h, n, sibling)
+
+    def whole_g(n):
+        for by in (0, -1, 1, 2):
+            for h in range(2):
+                g_wait(other(by), h, n)
 
     def grad_in_of(block):
         at = pl.ds(pl.multiple_of(block * rows, rows), rows)
-        total = lax.dot_general(G[at, 0:wide], w[0], NT, preferred_element_type=F32)
-        for c in range(1, 3):
-            total = total + lax.dot_general(
-                G[at, c * wide : (c + 1) * wide], w[c], NT, preferred_element_type=F32
-            )
+        total = lax.dot_general(G[0, at], w[0], NT, preferred_element_type=F32)
+        for n in range(1, CHUNKS):
+            total = total + lax.dot_general(G[n, at], w[n], NT, preferred_element_type=F32)
         return total
 
     def col_copy(block, side, h):
@@ -481,16 +491,13 @@
 
     def dw_at(q, h, m):
         return dw.at[
-            m // per,
-            pl.ds(pl.multiple_of(q * rows + h * half, half), half),
-            pl.ds((m % per) * step, step),
+            :, pl.ds(pl.multiple_of(q * rows + h * half, half), half), pl.ds(m * LANES, LANES)
         ]
 
     def multiply(m):
         for q in range(RING):
             D[q, m] = jnp.dot(
-                XT[q * rows : (q + 1) * rows, :], G[:, m * step : (m + 1) * step],
-                preferred_element_type=F32,
+                XT[q * rows : (q + 1) * rows, :], G[m], preferred_element_type=F32
             ).astype(BF16)
         out.start(D.at[to_o, m, top], xrel.at[0, m], xrel_sem.at[0, m], xr)
         out.start(D.at[to_o, m, bottom], xrel.at[1, m], xrel_sem.at[1, m], xl)
@@ -528,9 +535,10 @@
     def total_of(m):
         for h in range(2):
             arrived(zrec.at[m, halves[h]], zrec_sem.at[h, m], me)
-        dw[
-            m // per, pl.ds(pl.multiple_of(me.x * rows, rows), rows), pl.ds((m % per) * step, step)
-        ] = (S[m].astype(F32) + zrec[m].astype(F32)).astype(BF16)
+        total = (S[m].astype(F32) + zrec[m].astype(F32)).astype(BF16)
+        own_rows_x = pl.ds(pl.multiple_of(me.x * rows, rows), rows)
+        for c in range(3):
+            dw[c, own_rows_x, m * LANES : (m + 1) * LANES] = total[:, c * LANES : (c + 1) * LANES]
         gather(me.x, 0, m, xr)
         gather(me.x, 1, m, xl)
         gather(me.x, 1, m, xr)
@@ -549,6 +557,7 @@
         gathered(to_o, 1, m)
 
     stages = {
+        "F": projection, "H": channels, "A": relay_g, "B": share_g, "W": whole_g,
         "M": multiply, "X": relay_x, "E": exchange, "Z": relay_z, "T": total_of, "O": relay_out,
         "L": last_out, "C": col_round, "G": col_last,
     }
@@ -579,49 +588,54 @@
             for u in range(SUBS):
                 line_copy(j, u, col_down).wait_send()
 
-    for p in range(RING):
-        pair_copy(p).wait_send()
-    for n in range(6):
-        y_copy(n).wait_send()
+    for n in range(CHUNKS):
+        for p in range(RING):
+            pair_copy(p, n).wait_send()
+        for k in range(6):
+            y_copy(k, n).wait_send()
 
     @pl.when(me.row > 0)
     def _():
-        halo_copy(0).wait_send()
-        halo_copy(1).wait_send()
+        goa_copy.wait_send()
+        for n in range(CHUNKS):
+            halo_copy(0, n).wait_send()
 
     @pl.when(me.row < 7)
     def _():
-        halo_copy(2).wait_send()
-
-
-SENDS = 6 + 8 + CHUNKS * (4 + 2 + 2 + 2 + 4 + 2)
+        for n in range(CHUNKS):
+            halo_copy(1, n).wait_send()
+
+
+SENDS = CHUNKS * (6 + 8 + 4 + 2 + 2 + 2 + 4 + 2)
 
 
 def whole(tile, w, ft, it, go):
     rows, wide, deep = tile.shape[0], w.shape[2], w.shape[1]
-    half, step = rows // 2, 3 * wide // CHUNKS
+    half, step = rows // 2, 3 * LANES
     vmem, sem = pltpu.VMEM, pltpu.SemaphoreType.DMA
     return pl.pallas_call(
         whole_kernel,
         out_shape=(jax.ShapeDtypeStruct((rows, deep), BF16), jax.ShapeDtypeStruct(w.shape, BF16)),
         in_specs=[
-            pl.BlockSpec(memory_space=space) for space in (pl.ANY, pl.ANY, vmem, vmem, pl.ANY)
+            pl.BlockSpec(memory_space=pltpu.HBM) for _ in range(5)
         ],
         out_specs=(pl.BlockSpec(memory_space=pltpu.VMEM),) * 2,
         scratch_shapes=[
-            vmem(w.shape, BF16),
+            vmem((CHUNKS, deep, step), BF16),
+            vmem(ft.shape, F32),
+            vmem(it.shape, F32),
             vmem((rows, wide), BF16),
             vmem((8 * rows, deep), BF16),
             vmem((deep, 8 * rows), BF16),
-            vmem((RING, rows, 3 * wide), F32),
-            vmem((RING, rows, 3 * wide), BF16),
-            vmem((RING, rows, 3 * wide), BF16),
-            vmem((RING, rows, 3 * wide), BF16),
-            vmem((2, half, 3 * wide), BF16),
-            vmem((2, rows, 3 * wide), BF16),
-            vmem((rows + 2 * HALO, 3 * wide), BF16),
+            vmem((RING, CHUNKS, rows, step), F32),
+            vmem((RING, CHUNKS, rows, step), BF16),
+            vmem((RING, CHUNKS, rows, step), BF16),
+            vmem((RING, CHUNKS, rows, step), BF16),
+            vmem((2, CHUNKS, half, step), BF16),
+            vmem((2, CHUNKS, rows, step), BF16),
+            vmem((CHUNKS, rows + 2 * HALO, step), BF16),
             vmem((HALO, wide), BF16),
-            vmem((8 * rows, 3 * wide), BF16),
+            vmem((CHUNKS, 8 * rows, step), BF16),
             vmem((RING, CHUNKS, rows, step), BF16),
             vmem((2, CHUNKS, half, step), BF16),
             vmem((2, CHUNKS, rows, step), BF16),
@@ -631,19 +645,19 @@
             vmem((8, rows, deep), BF16),
             vmem((8, rows, deep), BF16),
             vmem((8, rows, deep), BF16),
-            sem((3,)),
+            sem((4 + 3 * CHUNKS,)),
             sem((SENDS,)),
             sem((9, SUBS)),
             sem((8, SUBS)),
-            sem((RING,)),
-            sem((RING,)),
-            sem((6,)),
-            sem((2,)),
-            sem((2, 2)),
-            sem((3,)),
-            sem((3,)),
+            sem((RING, CHUNKS)),
+            sem((RING, CHUNKS)),
+            sem((6, CHUNKS)),
+            sem((2, CHUNKS)),
+            sem((2, 2, CHUNKS)),
+            sem((3, CHUNKS)),
+            sem((3, CHUNKS)),
             sem((8, 2)),
-            sem((8, 2)),
+            sem((8, 2, CHUNKS)),
             sem((2, CHUNKS)),
             sem((2, 2, CHUNKS)),
             sem((2, CHUNKS)),

time: 161 us -> 158 us (0.981)
  the two profiles are of different devices: /device:TPU:32 before, /device:TPU:42 now
where the time goes in v4:
time: 158 us
  Pallas kernels  149 us (94%)
  local copies, waits for them, and re-layouts  5.32 us (3%)
  other arithmetic  2.11 us (1%)
    pallas_call x1, Pallas kernels, whole(): pl.pallas_call(whole_kernel, out_shape=(jax.ShapeDtypeStruct((rows, deep)...  149 us
    unnamed x11, local copies, waits for them, and re-layouts  5.32 us

profile of v4, /device:TPU:42, one launch (start us, length us, event | category | flops | bytes accessed | tf_op | source)
XLA Modules:
  0.0 157.5 jit_solution(4068169342175894183)
XLA Ops:
  0.6 0.0 copy-start
  0.6 1.4 copy-done
  2.0 0.0 copy-start.1
  2.0 0.9 copy-done.1
  2.9 0.0 copy-start.2
  2.9 0.9 copy-done.2
  3.8 0.0 copy-start.3
  3.9 0.7 copy-done.3
  4.6 0.0 copy-start.4
  4.6 0.7 copy-done.4
  5.3 149.5 %whole.1 = (bf16[128,512]{1,0:T(8,128)(2,1)S(1)}, bf16[3,512,512]{2,1,0:T(8,128)(2,1)S(1)}) custom-call(bf16[128,512]{1,0:T(8,128)(2,1)S(1)} %bitcast.7, bf16[3,512,512]{2,1,0:T(8,128)(2,1)S(1)} %bitcast.6, f32[3,3,512]{2,1,0:T(4,128)S(1)} %copy-done.3, f32[7,512]{1,0:T(8,128)S(1)} %copy-done.4, bf16[128,512]{1,0:T(8,128)(2,1)S(1)} %bitcast.8), custom_call_target="tpu_custom_call" | custom-call | tf_op jit(solution)/shard_map/whole/pallas_call | solution.py:616
  154.8 2.1 %convert_bitcast_fusion = f32[512,3,512]{2,0,1:T(8,128)} fusion(bf16[3,512,512]{2,1,0:T(8,128)(2,1)S(1)} %get-tuple-element.5), kind=kLoop, calls=%fused_computation | loop fusion | flops 786432 | bytes 4718592 | tf_op jit(solution)/shard_map/transpose | solution.py:680
  156.9 0.7 copy.8
Async XLA Ops:
  0.6 1.4 copy-start
  2.0 0.9 copy-start.1
  2.9 0.9 copy-start.2
  3.8 0.7 copy-start.3
  4.6 0.7 copy-start.4

commit v5 on v4

--- a/solution.py
+++ b/solution.py
@@ -13,10 +13,10 @@
 SUBS = 4
 RING = 4
 ORDER = (
-    "F0 F1 H0 F2", "H1 F3 H2 A0", "H3 A1 B0 A2", "B1 W0 M0 A3",
-    "B2 W1 M1 X0", "B3 E0 W2 M2", "X1 E1 W3 M3", "X2 E2 Z0 C0",
-    "X3 E3 Z1 C1", "Z2 C2 Z3 C3", "T0 C4 O0 T1", "C5 O1 L0 T2",
-    "C6 O2 L1 T3", "G0 O3 L2 L3",
+    "F3 F0 F1 F2", "H1 H2 H0 H3", "K0 M0 A0 A1", "X0 A2 A3 E0",
+    "B0 B1 W1 M1", "X1 B2 B3 E1", "W2 M2 X2 E2", "W3 M3 Z0 X3",
+    "E3 C0 Z1 C1", "T0 Z2 C2 O0", "Z3 C3 T1 C4", "O1 L0 C5 T2",
+    "O2 L1 C6 T3", "G0 O3 L2 L3",
 )
 F32 = jnp.float32
 BF16 = jnp.bfloat16
@@ -34,8 +34,11 @@
     def at_y(self, by):
         return (self.dp, ((self.y + by + RING) % RING) * 2 + self.core, self.col)
 
+    def in_row(self, by, core):
+        return (self.dp, ((self.y + by) % RING) * 2 + core, self.col)
+
     def sibling(self):
-        return (self.dp, self.y * 2 + 1 - self.core, self.col)
+        return self.in_row(0, 1 - self.core)
 
     def at_z(self, by):
         z = (self.zh * 8 + self.col + by + 16) % 16
@@ -75,9 +78,9 @@
 
 def whole_kernel(
     tile, w_hbm, ft_hbm, it_hbm, go_hbm, gx, dw,
-    w, ft, it, go, XG, XT, acc, psend, pair, Dy, yrel, yrec, win, goa,
+    w, ft, it, XG, XT, acc, psend, pair, Dy, yrel, yrec, win, ups,
     G, D, xrel, xrec, S, zrel, zrec, rr, rl, part,
-    fetch_sem, sends, ag_send, ag_recv, p_send, p_recv, y_send, yrel_sem, yrec_sem, h_send, h_recv,
+    fetch_sem, sends, ag_send, ag_recv, p_send, p_recv, y_send, yrel_sem, yrec_sem, h_send, h_recv, go_recv,
     col_send, g_recv, xrel_sem, xrec_sem, zrel_sem, zrec_sem, out_sem, rr_sem, rl_sem,
 ):
     me = Place()
@@ -89,58 +92,88 @@
     xr, xl = me.at_x(1), me.at_x(-1)
     up, down = me.at_z(4), me.at_z(-4)
     col_up, col_down = me.at_col(1), me.at_col(-1)
-    far = (me.dp, (me.row + 2 * me.core + 7) % 8, me.col)
+    others = [me.in_row(by, 1 - me.core) for by in (1, 2, 3)]
     own_rows = pl.ds(pl.multiple_of(me.col * rows, rows), rows)
     fetches = [
         pltpu.make_async_copy(tile, XG.at[own_rows], fetch_sem.at[0]),
-        pltpu.make_async_copy(go_hbm, go, fetch_sem.at[1]),
-        pltpu.make_async_copy(ft_hbm, ft, fetch_sem.at[2]),
-        pltpu.make_async_copy(it_hbm, it, fetch_sem.at[3]),
+        pltpu.make_async_copy(ft_hbm, ft, fetch_sem.at[1]),
+        pltpu.make_async_copy(it_hbm, it, fetch_sem.at[2]),
     ]
     for n in range(CHUNKS):
         for c in range(3):
             lanes, to = pl.ds(n * LANES, LANES), pl.ds(c * LANES, LANES)
             fetches.append(
                 pltpu.make_async_copy(
-                    w_hbm.at[c, :, lanes], w.at[n, :, to], fetch_sem.at[4 + 3 * n + c]
+                    w_hbm.at[c, :, lanes], w.at[n, :, to], fetch_sem.at[3 + 3 * n + c]
                 )
             )
     for copy in fetches:
         copy.start()
-    greet([right, left, sibling, far, xr, xl, up, down, col_up, col_down])
+    greet([right, left, me.at_y(2), sibling, *others, xr, xl, up, down, col_up, col_down])
     out = Sends(sends)
     top, bottom = pl.ds(0, half), pl.ds(half, half)
     halves = (top, bottom)
 
-    before, after = (me.dp, (me.row + 7) % 8, me.col), (me.dp, (me.row + 1) % 8, me.col)
-
-    goa_copy = pltpu.make_async_remote_copy(
-        src_ref=go_hbm.at[pl.ds(0, HALO)], dst_ref=goa, send_sem=h_send.at[2, 0],
-        recv_sem=h_recv.at[2, 0], device_id=before, device_id_type=MESH,
+    span = 4 * rows
+    token_half = me.y // 2
+
+    def go_part(by, head):
+        n = (me.y + by) % RING
+        lanes = pl.ds(pl.multiple_of(n * LANES, LANES), LANES)
+        slot = me.row % 4
+        if head:
+            src, dst = go_hbm.at[pl.ds(0, HALO), lanes], ups.at[pl.ds(HALO + span, HALO)]
+            recv, device = go_recv.at[4], me.in_row(by, 0)
+        else:
+            src = go_hbm.at[:, lanes]
+            dst = ups.at[pl.ds(pl.multiple_of(HALO + slot * rows, HALO), rows)]
+            recv, device = go_recv.at[slot], me.in_row(by, token_half)
+        remote = pltpu.make_async_remote_copy(
+            src_ref=src, dst_ref=dst, send_sem=h_send.at[2 + by + 4 * head], recv_sem=recv,
+            device_id=device, device_id_type=MESH,
+        )
+        return remote, pltpu.make_async_copy(src, dst, recv)
+
+    stays = token_half == me.core
+    has_head = me.row == 4
+    for by in range(RING):
+        remote, local = go_part(by, 0)
+        if by:
+            remote.start()
+        else:
+
+            @pl.when(stays)
+            def _():
+                local.start()
+
+            @pl.when(jnp.logical_not(stays))
+            def _():
+                remote.start()
+
+        remote_head, local_head = go_part(by, 1)
+
+        @pl.when(has_head)
+        def _():
+            (remote_head if by else local_head).start()
+
+    ups[0:HALO, :] = jnp.zeros((HALO, LANES), BF16)
+
+    @pl.when(me.core == 0)
+    def _():
+        win[0:HALO, :] = jnp.zeros((HALO, step), BF16)
+
+    @pl.when(me.core == 1)
+    def _():
+        win[span + HALO :, :] = jnp.zeros((HALO, step), BF16)
+        ups[span + HALO :, :] = jnp.zeros((HALO, LANES), BF16)
+
+    tail_copy, head_copy = (
+        pltpu.make_async_remote_copy(
+            src_ref=win.at[pl.ds(src, HALO)], dst_ref=win.at[pl.ds(dst, HALO)],
+            send_sem=h_send.at[k], recv_sem=h_recv.at[k], device_id=sibling, device_id_type=MESH,
+        )
+        for k, (src, dst) in enumerate(((span, 0), (HALO, span + HALO)))
     )
-
-    def halo_copy(side, n):
-        src, dst, device = (
-            (pl.ds(HALO, HALO), pl.ds(rows + HALO, HALO), before),
-            (pl.ds(rows, HALO), pl.ds(0, HALO), after),
-        )[side]
-        return pltpu.make_async_remote_copy(
-            src_ref=win.at[n, src], dst_ref=win.at[n, dst], send_sem=h_send.at[side, n],
-            recv_sem=h_recv.at[side, n], device_id=device, device_id_type=MESH,
-        )
-
-    @pl.when(me.row > 0)
-    def _():
-        goa_copy.start()
-
-    @pl.when(me.row == 0)
-    def _():
-        win[:, 0:HALO, :] = jnp.zeros((CHUNKS, HALO, step), BF16)
-
-    @pl.when(me.row == 7)
-    def _():
-        win[:, rows + HALO :, :] = jnp.zeros((CHUNKS, HALO, step), BF16)
-        goa[...] = jnp.zeros_like(goa)
 
     def block_at(j):
         return pl.ds(pl.multiple_of(j * rows, rows), rows)
@@ -177,101 +210,72 @@
     for copy in fetches:
         copy.wait()
 
-    def pair_copy(p, n):
+    def pair_copy(s, n):
         return pltpu.make_async_remote_copy(
-            src_ref=psend.at[p, n], dst_ref=pair.at[p, n], send_sem=p_send.at[p, n],
-            recv_sem=p_recv.at[p, n], device_id=sibling, device_id_type=MESH,
-        )
+            src_ref=psend.at[s, n], dst_ref=pair.at[s, n], send_sem=p_send.at[s, n],
+            recv_sem=p_recv.at[s, n], device_id=sibling, device_id_type=MESH,
+        )
+
+    y_opp, y_r, y_l = ((me.y + by) % RING for by in (2, 1, 3))
 
     def project(j):
         x = XG[block_at(j), :]
-        p = j // 2
-        mine = j % 2 == me.core
-        for n in range(CHUNKS):
+        s = j % 4
+        mine = j // 4 == me.core
+        for n in (y_opp, y_r, y_l, me.y):
             product = jnp.dot(x, w[n], preferred_element_type=F32)
 
             @pl.when(mine)
             def _():
-                acc[p, n] = product
+                acc[s, n] = product
 
             @pl.when(jnp.logical_not(mine))
             def _():
-                psend[p, n] = product.astype(BF16)
-                pair_copy(p, n).start()
+                psend[s, n] = product.astype(BF16)
+                pair_copy(s, n).start()
 
         XT[:, block_at(j)] = x.T
 
-    y_opp, y_r, y_l = ((me.y + by) % RING for by in (2, 1, 3))
-
-    def y_copy(k, n):
+    def y_copy(k, s):
         src, dst, sem, device = (
-            (Dy.at[y_opp, n, top], yrel.at[0, n], yrel_sem.at[0, n], right),
-            (Dy.at[y_opp, n, bottom], yrel.at[1, n], yrel_sem.at[1, n], left),
-            (Dy.at[y_r, n, bottom], yrec.at[0, n, bottom], yrec_sem.at[0, 1, n], right),
-            (Dy.at[y_l, n, top], yrec.at[1, n, top], yrec_sem.at[1, 0, n], left),
-            (Dy.at[y_r, n, top], yrec.at[0, n, top], yrec_sem.at[0, 0, n], right),
-            (Dy.at[y_l, n, bottom], yrec.at[1, n, bottom], yrec_sem.at[1, 1, n], left),
+            (Dy.at[s, y_opp, top], yrel.at[0, s], yrel_sem.at[0, s], right),
+            (Dy.at[s, y_opp, bottom], yrel.at[1, s], yrel_sem.at[1, s], left),
+            (Dy.at[s, y_r, bottom], yrec.at[0, s, bottom], yrec_sem.at[0, 1, s], right),
+            (Dy.at[s, y_l, top], yrec.at[1, s, top], yrec_sem.at[1, 0, s], left),
+            (Dy.at[s, y_r, top], yrec.at[0, s, top], yrec_sem.at[0, 0, s], right),
+            (Dy.at[s, y_l, bottom], yrec.at[1, s, bottom], yrec_sem.at[1, 1, s], left),
         )[k]
         return pltpu.make_async_remote_copy(
-            src_ref=src, dst_ref=dst, send_sem=y_send.at[k, n], recv_sem=sem, device_id=device,
+            src_ref=src, dst_ref=dst, send_sem=y_send.at[k, s], recv_sem=sem, device_id=device,
             device_id_type=MESH,
         )
 
-    def piece(d):
-        sign = (2 * (d % 2) - 1) * (1 - 2 * (me.col % 2))
-        p = me.col // 2 + sign * (d // 2)
-        return p, jnp.logical_and(jnp.logical_and(p >= 0, p < RING), jnp.logical_and(d >= 1, d <= 7))
-
-    def pair_sum(d):
-        p, there = piece(d)
-        role = (p - me.y + RING) % RING
-
-        for n in range(CHUNKS):
+    def pair_sum(s):
+        for n, copies in ((y_opp, (0, 1)), (y_r, (2,)), (y_l, (3,)), (me.y, ())):
+            arrived(pair.at[s, n], p_recv.at[s, n], me)
+            total = acc[s, n] + pair[s, n].astype(F32)
+            if copies:
+                Dy[s, n] = total.astype(BF16)
+                for k in copies:
+                    y_copy(k, s).start()
+            else:
+                acc[s, n] = total
+
+    def relay_y(s):
+        for side, n, at, k in ((0, y_r, top, 4), (1, y_l, bottom, 5)):
+            arrived(yrel.at[side, s], yrel_sem.at[side, s], me)
+            Dy[s, n, at] = (Dy[s, n, at].astype(F32) + yrel[side, s].astype(F32)).astype(BF16)
+            y_copy(k, s).start()
+
+    def for_kept(stage, d):
+        for side in (-1, 1):
+            j = me.col + side * d
+            there = jnp.logical_and(jnp.logical_and(j >= 0, j <= 7), d >= (side + 1) // 2)
+            there = jnp.logical_and(there, (j + 8) // 4 - 2 == me.core)
 
             @pl.when(there)
             def _():
-                arrived(pair.at[p, n], p_recv.at[p, n], me)
-
-            @pl.when(jnp.logical_and(there, role == 0))
-            def _():
-                acc[p, n] = acc[p, n] + pair[p, n].astype(F32)
-
-            @pl.when(jnp.logical_and(there, role != 0))
-            def _():
-                Dy[p, n] = (acc[p, n] + pair[p, n].astype(F32)).astype(BF16)
-
-            @pl.when(jnp.logical_and(there, role == 2))
-            def _():
-                y_copy(0, n).start()
-                y_copy(1, n).start()
-
-            @pl.when(jnp.logical_and(there, role == 1))
-            def _():
-                y_copy(2, n).start()
-
-            @pl.when(jnp.logical_and(there, role == 3))
-            def _():
-                y_copy(3, n).start()
-
-    def relay_y(d):
-        p, there = piece(d)
-        role = (p - me.y + RING) % RING
-
-        @pl.when(jnp.logical_and(there, role == 1))
-        def _():
-            for n in range(CHUNKS):
-                arrived(yrel.at[0, n], yrel_sem.at[0, n], me)
-                Dy[p, n, top] = (Dy[p, n, top].astype(F32) + yrel[0, n].astype(F32)).astype(BF16)
-                y_copy(4, n).start()
-
-        @pl.when(jnp.logical_and(there, role == 3))
-        def _():
-            for n in range(CHUNKS):
-                arrived(yrel.at[1, n], yrel_sem.at[1, n], me)
-                Dy[p, n, bottom] = (
-                    Dy[p, n, bottom].astype(F32) + yrel[1, n].astype(F32)
-                ).astype(BF16)
-                y_copy(5, n).start()
+                stage(j % 4)
 
     def pass_on(d, some):
         @pl.when(jnp.logical_and(d <= 7, me.col - d >= 0))
@@ -308,26 +312,29 @@
         def _():
             project(me.col + last)
 
-        relay_y(d - 3)
-        pair_sum(d - 2)
+        for_kept(relay_y, d - 3)
+        for_kept(pair_sum, d - 2)
         return carry
 
     lax.fori_loop(1, 11, line_step, 0)
 
-    def projection(n):
+    def projection(s):
         for side in range(2):
             for h in range(2):
-                arrived(yrec.at[side, n, halves[h]], yrec_sem.at[side, h, n], me)
-        total = acc[me.y, n] + yrec[0, n].astype(F32) + yrec[1, n].astype(F32)
-        win[n, HALO : rows + HALO, :] = total.astype(BF16)
-
-        @pl.when(me.row > 0)
-        def _():
-            halo_copy(0, n).start()
-
-        @pl.when(me.row < 7)
-        def _():
-            halo_copy(1, n).start()
+                arrived(yrec.at[side, s, halves[h]], yrec_sem.at[side, h, s], me)
+        total = acc[s, me.y] + yrec[0, s].astype(F32) + yrec[1, s].astype(F32)
+        win[HALO + s * rows : HALO + (s + 1) * rows, :] = total.astype(BF16)
+        if s == 3:
+
+            @pl.when(me.core == 0)
+            def _():
+                tail_copy.start()
+
+        if s == 0:
+
+            @pl.when(me.core == 1)
+            def _():
+                head_copy.start()
 
     length = rows + 2 * HALO
 
@@ -343,57 +350,63 @@
             total = total + taps[lag] * pltpu.roll(seq, length - lag, 0)
         return total
 
-    own_block = block_at(me.row)
-
-    def channels(n):
-        @pl.when(me.row > 0)
-        def _():
-            arrived(win.at[n, pl.ds(0, HALO)], h_recv.at[1, n], me)
-
-        @pl.when(me.row < 7)
-        def _():
-            arrived(win.at[n, pl.ds(rows + HALO, HALO)], h_recv.at[0, n], me)
-
-            if n == 0:
-                arrived(goa, h_recv.at[2, 0], me)
-
-        lanes = slice(n * LANES, (n + 1) * LANES)
+    def take_grad_out():
+        for s in range(4):
+            arrived(ups.at[pl.ds(HALO + s * rows, rows)], go_recv.at[s], me)
+
+        @pl.when(me.core == 0)
+        def _():
+            arrived(ups.at[pl.ds(HALO + span, HALO)], go_recv.at[4], me)
+
+    def channels(s):
+        if s == 1:
+            take_grad_out()
+        if s == 0:
+
+            @pl.when(me.core == 1)
+            def _():
+                arrived(win.at[pl.ds(0, HALO)], h_recv.at[0], me)
+
+        if s == 3:
+
+            @pl.when(me.core == 0)
+            def _():
+                arrived(win.at[pl.ds(span + HALO, HALO)], h_recv.at[1], me)
+
+        lanes = pl.ds(pl.multiple_of(me.y * LANES, LANES), LANES)
         parts = [slice(c * LANES, (c + 1) * LANES) for c in range(3)]
-        taps = [[ft[s, c : c + 1, lanes] for s in range(3)] for c in range(3)]
-        inner_taps = [it[s : s + 1, lanes] for s in range(7)]
-        query, key, value = (causal(win[n, :, parts[c]].astype(F32), taps[c]) for c in range(3))
-        upstream = jnp.concatenate(
-            [jnp.zeros((HALO, LANES), F32), go[:, lanes].astype(F32), goa[:, lanes].astype(F32)],
-            axis=0,
-        )
+        taps = [[ft[k, c : c + 1, lanes] for k in range(3)] for c in range(3)]
+        inner_taps = [it[k : k + 1, lanes] for k in range(7)]
+        tokens = slice(s * rows, s * rows + length)
+        query, key, value = (
+            causal(win[tokens, parts[c]].astype(F32), taps[c]) for c in range(3)
+        )
+        upstream = ups[tokens, :].astype(F32)
         product = (key * value).astype(BF16).astype(F32)
         inner = causal(product, inner_taps)
         grad_product = anticausal(upstream * query, inner_taps)
         mixed = (upstream * inner, grad_product * value, grad_product * key)
+        at = pl.ds(pl.multiple_of(me.core * span + s * rows, rows), rows)
         for c in range(3):
             grad = anticausal(mixed[c], taps[c])
-            G[n, own_block, parts[c]] = grad[HALO : rows + HALO].astype(BF16)
-        g_send(me.row, 0, n, right)
-        g_send(me.row, 1, n, left)
-        g_send(me.row, 1, n, right)
-        g_send(me.row, 0, n, left)
+            G[me.y, at, parts[c]] = grad[HALO : rows + HALO].astype(BF16)
         for h in range(2):
-            g_send(me.row, h, n, sibling)
-
-    def g_at(slot, h, n):
-        return G.at[n, pl.ds(pl.multiple_of(slot * rows + h * half, half), half)]
-
-    def g_send(slot, h, n, device):
-        out.start(g_at(slot, h, n), g_at(slot, h, n), g_recv.at[slot, h, n], device)
-
-    def g_wait(slot, h, n):
-        arrived(g_at(slot, h, n), g_recv.at[slot, h, n], me)
-
-    def same(by):
-        return ((me.y + by + RING) % RING) * 2 + me.core
-
-    def other(by):
-        return ((me.y + by + RING) % RING) * 2 + 1 - me.core
+            g_send(me.y, h, s, sibling)
+        g_send(me.y, 0, s, right)
+        g_send(me.y, 1, s, left)
+        g_send(me.y, 1, s, right)
+        g_send(me.y, 0, s, left)
+
+    def g_at(n, core, h, s):
+        first = core * span + s * rows + h * half
+        return G.at[n, pl.ds(pl.multiple_of(first, half), half)]
+
+    def g_send(n, h, s, device):
+        at = g_at(n, me.core, h, s)
+        out.start(at, at, g_recv.at[n * 2 + me.core, h, s], device)
+
+    def g_wait(n, core, h, s):
+        arrived(g_at(n, core, h, s), g_recv.at[n * 2 + core, h, s], me)
 
     @pl.when(me.col == 7)
     def _():
@@ -403,27 +416,29 @@
     def _():
         rl[...] = jnp.zeros_like(rl)
 
-    def relay_g(n):
-        g_wait(same(-1), 0, n)
-        g_send(same(-1), 0, n, right)
-        g_send(same(-1), 0, n, sibling)
-        g_wait(same(1), 1, n)
-        g_send(same(1), 1, n, left)
-        g_send(same(1), 1, n, sibling)
-        g_wait(same(-1), 1, n)
-        g_send(same(-1), 1, n, sibling)
-        g_wait(same(1), 0, n)
-        g_send(same(1), 0, n, sibling)
-
-    def share_g(n):
+    def relay_g(s):
+        g_wait(y_l, me.core, 0, s)
+        g_send(y_l, 0, s, right)
+        g_send(y_l, 0, s, sibling)
+        g_wait(y_r, me.core, 1, s)
+        g_send(y_r, 1, s, left)
+        g_send(y_r, 1, s, sibling)
+        g_wait(y_l, me.core, 1, s)
+        g_send(y_l, 1, s, sibling)
+        g_wait(y_r, me.core, 0, s)
+        g_send(y_r, 0, s, sibling)
+
+    def share_g(s):
         for h in range(2):
-            g_wait(same(2), h, n)
-            g_send(same(2), h, n, sibling)
-
-    def whole_g(n):
-        for by in (0, -1, 1, 2):
+            g_wait(y_opp, me.core, h, s)
+            g_send(y_opp, h, s, sibling)
+
+    chunk = (me.y, y_r, y_l, y_opp)
+
+    def whole_g(k):
+        for s in range(4):
             for h in range(2):
-                g_wait(other(by), h, n)
+                g_wait(chunk[k], 1 - me.core, h, s)
 
     def grad_in_of(block):
         at = pl.ds(pl.multiple_of(block * rows, rows), rows)
@@ -489,15 +504,18 @@
 
     to_r, to_l, to_o = ((me.x + by + RING) % RING for by in (1, 3, 2))
 
+    def lanes_of(m):
+        return pl.ds(pl.multiple_of(chunk[m] * LANES, LANES), LANES)
+
     def dw_at(q, h, m):
         return dw.at[
-            :, pl.ds(pl.multiple_of(q * rows + h * half, half), half), pl.ds(m * LANES, LANES)
+            :, pl.ds(pl.multiple_of(q * rows + h * half, half), half), lanes_of(m)
         ]
 
     def multiply(m):
         for q in range(RING):
             D[q, m] = jnp.dot(
-                XT[q * rows : (q + 1) * rows, :], G[m], preferred_element_type=F32
+                XT[q * rows : (q + 1) * rows, :], G[chunk[m]], preferred_element_type=F32
             ).astype(BF16)
         out.start(D.at[to_o, m, top], xrel.at[0, m], xrel_sem.at[0, m], xr)
         out.start(D.at[to_o, m, bottom], xrel.at[1, m], xrel_sem.at[1, m], xl)
@@ -538,7 +556,7 @@
         total = (S[m].astype(F32) + zrec[m].astype(F32)).astype(BF16)
         own_rows_x = pl.ds(pl.multiple_of(me.x * rows, rows), rows)
         for c in range(3):
-            dw[c, own_rows_x, m * LANES : (m + 1) * LANES] = total[:, c * LANES : (c + 1) * LANES]
+            dw[c, own_rows_x, lanes_of(m)] = total[:, c * LANES : (c + 1) * LANES]
         gather(me.x, 0, m, xr)
         gather(me.x, 1, m, xl)
         gather(me.x, 1, m, xr)
@@ -557,7 +575,7 @@
         gathered(to_o, 1, m)
 
     stages = {
-        "F": projection, "H": channels, "A": relay_g, "B": share_g, "W": whole_g,
+        "F": projection, "H": channels, "A": relay_g, "B": share_g, "K": whole_g, "W": whole_g,
         "M": multiply, "X": relay_x, "E": exchange, "Z": relay_z, "T": total_of, "O": relay_out,
         "L": last_out, "C": col_round, "G": col_last,
     }
@@ -594,23 +612,34 @@
         for k in range(6):
             y_copy(k, n).wait_send()
 
-    @pl.when(me.row > 0)
-    def _():
-        goa_copy.wait_send()
-        for n in range(CHUNKS):
-            halo_copy(0, n).wait_send()
-
-    @pl.when(me.row < 7)
-    def _():
-        for n in range(CHUNKS):
-            halo_copy(1, n).wait_send()
+    @pl.when(me.core == 0)
+    def _():
+        tail_copy.wait_send()
+
+    @pl.when(me.core == 1)
+    def _():
+        head_copy.wait_send()
+
+    for by in range(RING):
+        if by:
+            go_part(by, 0)[0].wait_send()
+
+            @pl.when(has_head)
+            def _():
+                go_part(by, 1)[0].wait_send()
+
+        else:
+
+            @pl.when(jnp.logical_not(stays))
+            def _():
+                go_part(0, 0)[0].wait_send()
 
 
 SENDS = CHUNKS * (6 + 8 + 4 + 2 + 2 + 2 + 4 + 2)
 
 
 def whole(tile, w, ft, it, go):
-    rows, wide, deep = tile.shape[0], w.shape[2], w.shape[1]
+    rows, deep = tile.shape[0], w.shape[1]
     half, step = rows // 2, 3 * LANES
     vmem, sem = pltpu.VMEM, pltpu.SemaphoreType.DMA
     return pl.pallas_call(
@@ -624,7 +653,6 @@
             vmem((CHUNKS, deep, step), BF16),
             vmem(ft.shape, F32),
             vmem(it.shape, F32),
-            vmem((rows, wide), BF16),
             vmem((8 * rows, deep), BF16),
             vmem((deep, 8 * rows), BF16),
             vmem((RING, CHUNKS, rows, step), F32),
@@ -633,8 +661,8 @@
             vmem((RING, CHUNKS, rows, step), BF16),
             vmem((2, CHUNKS, half, step), BF16),
             vmem((2, CHUNKS, rows, step), BF16),
-            vmem((CHUNKS, rows + 2 * HALO, step), BF16),
-            vmem((HALO, wide), BF16),
+            vmem((4 * rows + 2 * HALO, step), BF16),
+            vmem((4 * rows + 2 * HALO, LANES), BF16),
             vmem((CHUNKS, 8 * rows, step), BF16),
             vmem((RING, CHUNKS, rows, step), BF16),
             vmem((2, CHUNKS, half, step), BF16),
@@ -645,7 +673,7 @@
             vmem((8, rows, deep), BF16),
             vmem((8, rows, deep), BF16),
             vmem((8, rows, deep), BF16),
-            sem((4 + 3 * CHUNKS,)),
+            sem((3 + 3 * CHUNKS,)),
             sem((SENDS,)),
             sem((9, SUBS)),
             sem((8, SUBS)),
@@ -654,8 +682,9 @@
             sem((6, CHUNKS)),
             sem((2, CHUNKS)),
             sem((2, 2, CHUNKS)),
-            sem((3, CHUNKS)),
-            sem((3, CHUNKS)),
+            sem((10,)),
+            sem((2,)),
+            sem((5,)),
             sem((8, 2)),
             sem((8, 2, CHUNKS)),
             sem((2, CHUNKS)),
@@ -667,7 +696,7 @@
             sem((8, 2)),
         ],
         compiler_params=pltpu.CompilerParams(
-            collective_id=1, has_side_effects=True, vmem_limit_bytes=50 * 2**20
+            collective_id=1, has_side_effects=True, vmem_limit_bytes=63 * 2**20
         ),
         name="whole",
     )(tile, w, ft, it, go)

time: 158 us -> 145 us (0.918)
  the two profiles are of different devices: /device:TPU:42 before, /device:TPU:58 now
where the time goes in v5:
time: 145 us
  Pallas kernels  140 us (97%)
  other arithmetic  3.55 us (2%)
    pallas_call x1, Pallas kernels, whole(): pl.pallas_call(whole_kernel, out_shape=(jax.ShapeDtypeStruct((rows, deep)...  140 us
    transpose x1, other arithmetic, on_device(): return (grad_x[None], grad_w.astype(F32).transpose(1, 0, 2))  3.55 us

profile of v5, /device:TPU:58, one launch (start us, length us, event | category | flops | bytes accessed | tf_op | source)
XLA Modules:
  0.0 144.5 jit_solution(4967370379868038087)
XLA Ops:
  0.6 139.7 %whole.1 = (bf16[128,512]{1,0:T(8,128)(2,1)}, bf16[3,512,512]{2,1,0:T(8,128)(2,1)}) custom-call(bf16[128,512]{1,0:T(8,128)(2,1)} %bitcast.7, bf16[3,512,512]{2,1,0:T(8,128)(2,1)} %bitcast.6, f32[3,3,512]{2,1,0:T(4,128)} %ft_hbm.1, f32[7,512]{1,0:T(8,128)} %it_hbm.1, bf16[128,512]{1,0:T(8,128)(2,1)} %bitcast.8), custom_call_target="tpu_custom_call" | custom-call | tf_op jit(solution)/shard_map/whole/pallas_call | solution.py:645
  140.3 0.0 copy-start
  140.3 3.5 %convert_bitcast_fusion = f32[512,3,512]{2,0,1:T(8,128)} fusion(bf16[3,512,512]{2,1,0:T(8,128)(2,1)} %get-tuple-element.5), kind=kLoop, calls=%fused_computation | loop fusion | flops 786432 | bytes 4718592 | tf_op jit(solution)/shard_map/transpose | solution.py:709
  143.9 0.0 copy-done
  143.9 0.7 copy.8
Async XLA Ops:
  140.3 3.6 %copy-start = (bf16[128,512]{1,0:T(8,128)(2,1)S(1)}, bf16[128,512]{1,0:T(8,128)(2,1)}, u32[]{:S(2)}) copy-start(bf16[128,512]{1,0:T(8,128)(2,1)} %get-tuple-element.4) | copy-start | bytes 393220

commit v6 on v5

--- a/solution.py
+++ b/solution.py
@@ -13,10 +13,10 @@
 SUBS = 4
 RING = 4
 ORDER = (
-    "F3 F0 F1 F2", "H1 H2 H0 H3", "K0 M0 A0 A1", "X0 A2 A3 E0",
-    "B0 B1 W1 M1", "X1 B2 B3 E1", "W2 M2 X2 E2", "W3 M3 Z0 X3",
-    "E3 C0 Z1 C1", "T0 Z2 C2 O0", "Z3 C3 T1 C4", "O1 L0 C5 T2",
-    "O2 L1 C6 T3", "G0 O3 L2 L3",
+    "F3 F0 F1 F2", "H1 H2 H0 H3", "K0 M0 A0 X0", "A1 A2 A3 E0",
+    "B0 B1 W1 M1", "X1 B2 B3 E1", "W2 M2 Z0 X2", "W3 M3 E2 X3",
+    "Z1 E3 C0 Z2", "T0 C1 O0 Z3", "C2 L0 T1 C3", "O1 T2 C4 L1",
+    "O2 C5 T3 C6", "O3 L2 G0 L3",
 )
 F32 = jnp.float32
 BF16 = jnp.bfloat16

time: 145 us -> 137 us (0.945)
  the two profiles are of different devices: /device:TPU:58 before, /device:TPU:32 now
where the time goes in v6:
time: 137 us
  Pallas kernels  132 us (96%)
  other arithmetic  3.55 us (3%)
    pallas_call x1, Pallas kernels, whole(): pl.pallas_call(whole_kernel, out_shape=(jax.ShapeDtypeStruct((rows, deep)...  132 us
    transpose x1, other arithmetic, on_device(): return (grad_x[None], grad_w.astype(F32).transpose(1, 0, 2))  3.55 us

profile of v6, /device:TPU:32, one launch (start us, length us, event | category | flops | bytes accessed | tf_op | source)
XLA Modules:
  0.0 137.2 jit_solution(4165096125009004617)
XLA Ops:
  0.6 132.3 %whole.1 = (bf16[128,512]{1,0:T(8,128)(2,1)}, bf16[3,512,512]{2,1,0:T(8,128)(2,1)}) custom-call(bf16[128,512]{1,0:T(8,128)(2,1)} %bitcast.7, bf16[3,512,512]{2,1,0:T(8,128)(2,1)} %bitcast.6, f32[3,3,512]{2,1,0:T(4,128)} %ft_hbm.1, f32[7,512]{1,0:T(8,128)} %it_hbm.1, bf16[128,512]{1,0:T(8,128)(2,1)} %bitcast.8), custom_call_target="tpu_custom_call" | custom-call | tf_op jit(solution)/shard_map/whole/pallas_call | solution.py:645
  133.0 0.0 copy-start
  133.0 3.5 %convert_bitcast_fusion = f32[512,3,512]{2,0,1:T(8,128)} fusion(bf16[3,512,512]{2,1,0:T(8,128)(2,1)} %get-tuple-element.5), kind=kLoop, calls=%fused_computation | loop fusion | flops 786432 | bytes 4718592 | tf_op jit(solution)/shard_map/transpose | solution.py:709
  136.5 0.0 copy-done
  136.5 0.7 copy.8
Async XLA Ops:
  133.0 3.6 %copy-start = (bf16[128,512]{1,0:T(8,128)(2,1)S(1)}, bf16[128,512]{1,0:T(8,128)(2,1)}, u32[]{:S(2)}) copy-start(bf16[128,512]{1,0:T(8,128)(2,1)} %get-tuple-element.4) | copy-start | bytes 393220

commit v7 on v6

--- a/solution.py
+++ b/solution.py
@@ -696,10 +696,10 @@
             sem((8, 2)),
         ],
         compiler_params=pltpu.CompilerParams(
-            collective_id=1, has_side_effects=True, vmem_limit_bytes=63 * 2**20
+            collective_id=1, has_side_effects=True, vmem_limit_bytes=52 * 2**20
         ),
         name="whole",
-    )(tile, w, ft, it, go)
+    )(*(pltpu.with_memory_space_constraint(a, pltpu.HBM) for a in (tile, w, ft, it, go)))
 
 
 def on_device(inputs, weights, feature_taps, inner_taps, grad_out):

time: 137 us -> 134 us (0.978)
  Pallas kernels: 132 us -> 130 us
  other arithmetic: 3.55 us -> 2.11 us
    pallas_call x1, Pallas kernels: 132 us -> 130 us  [whole(): pl.pallas_call(whole_kernel, out_shape=(jax.ShapeDtypeStruct((rows, deep)...]
    transpose x1, other arithmetic: 3.55 us -> 2.11 us  [on_device(): return (grad_x[None], grad_w.astype(F32).transpose(1, 0, 2))]
where the time goes in v7:
time: 134 us
  Pallas kernels  130 us (97%)
  other arithmetic  2.11 us (2%)
    pallas_call x1, Pallas kernels, whole(): pl.pallas_call(whole_kernel, out_shape=(jax.ShapeDtypeStruct((rows, deep)...  130 us

profile of v7, /device:TPU:32, one launch (start us, length us, event | category | flops | bytes accessed | tf_op | source)
XLA Modules:
  0.0 133.8 jit_solution(10224915903106692814)
XLA Ops:
  0.6 130.4 %whole.1 = (bf16[128,512]{1,0:T(8,128)(2,1)S(1)}, bf16[3,512,512]{2,1,0:T(8,128)(2,1)S(1)}) custom-call(bf16[128,512]{1,0:T(8,128)(2,1)} %bitcast.8, bf16[3,512,512]{2,1,0:T(8,128)(2,1)} %bitcast.7, f32[3,3,512]{2,1,0:T(4,128)} %ft_hbm.1, f32[7,512]{1,0:T(8,128)} %it_hbm.1, bf16[128,512]{1,0:T(8,128)(2,1)} %bitcast.9), custom_call_target="tpu_custom_call" | custom-call | tf_op jit(solution)/shard_map/whole/pallas_call | solution.py:645
  131.0 2.1 %convert_bitcast_fusion = f32[512,3,512]{2,0,1:T(8,128)} fusion(bf16[3,512,512]{2,1,0:T(8,128)(2,1)S(1)} %get-tuple-element.5), kind=kLoop, calls=%fused_computation | loop fusion | flops 786432 | bytes 4718592 | tf_op jit(solution)/shard_map/transpose | solution.py:709
  133.1 0.7 copy.8

commit v8 on v7

--- a/solution.py
+++ b/solution.py
@@ -10,7 +10,7 @@
 CHUNKS = 4
 HALO = 16
 LANES = 128
-SUBS = 4
+SUBS = 2
 RING = 4
 ORDER = (
     "F3 F0 F1 F2", "H1 H2 H0 H3", "K0 M0 A0 X0", "A1 A2 A3 E0",

time: 134 us -> 135 us (level)
  no operation moved by 1% of the time
where the time goes in v8:
time: 135 us
  Pallas kernels  131 us (97%)
  other arithmetic  2.11 us (2%)
    pallas_call x1, Pallas kernels, whole(): pl.pallas_call(whole_kernel, out_shape=(jax.ShapeDtypeStruct((rows, deep)...  131 us

profile of v8, /device:TPU:32, one launch (start us, length us, event | category | flops | bytes accessed | tf_op | source)
XLA Modules:
  0.0 134.9 jit_solution(11360048424178239968)
XLA Ops:
  0.6 131.5 %whole.1 = (bf16[128,512]{1,0:T(8,128)(2,1)S(1)}, bf16[3,512,512]{2,1,0:T(8,128)(2,1)S(1)}) custom-call(bf16[128,512]{1,0:T(8,128)(2,1)} %bitcast.8, bf16[3,512,512]{2,1,0:T(8,128)(2,1)} %bitcast.7, f32[3,3,512]{2,1,0:T(4,128)} %ft_hbm.1, f32[7,512]{1,0:T(8,128)} %it_hbm.1, bf16[128,512]{1,0:T(8,128)(2,1)} %bitcast.9), custom_call_target="tpu_custom_call" | custom-call | tf_op jit(solution)/shard_map/whole/pallas_call | solution.py:645
  132.1 2.1 %convert_bitcast_fusion = f32[512,3,512]{2,0,1:T(8,128)} fusion(bf16[3,512,512]{2,1,0:T(8,128)(2,1)S(1)} %get-tuple-element.5), kind=kLoop, calls=%fused_computation | loop fusion | flops 786432 | bytes 4718592 | tf_op jit(solution)/shard_map/transpose | solution.py:709
  134.2 0.7 copy.8
